TPU v7x, 512 devices: a whole 4x4x16 slice. The times are simulated.
512 devices in a mesh: dom: 64 (over x, z), rep: 8 (over y, core).
Axes of the slice: x: 4, y: 4, z: 16, core: 2. Of those that a mesh axis runs over, the one named last changes fastest.
Arguments:
- features: bfloat16 [65536, 256], P(('dom', 'rep')), may hold values from -6 to 6
- block_values: bfloat16 [512, 16, 8, 128, 128], P(('dom', 'rep'))
- block_columns: int32 [512, 16, 8], P(('dom', 'rep')), may hold values from 0 to 63, as said below
- weight: bfloat16 [256, 256], replicated, may hold values from -0.375 to 0.375
- cotangent: bfloat16 [65536, 256], P(('dom', 'rep')), may hold values from -6 to 6
Outputs:
- feature_grad: bfloat16 [65536, 256], P(('dom', 'rep'))
- weight_grad: float32 [256, 256], replicated
Inputs may be any that keep to these rules, and one draw needn't show every extreme that they name: Slot (t, a) of the device with dom index d and rep index r lies at block row d * 8 + a and block column block_columns * 8 + r. The adjacency is symmetric: each slot at block row p and block column q has a partner slot of the same t at block row q and block column p whose block_values are its transpose; a slot with p equal to q holds a symmetric block.
All inputs are finite; a program needn't handle non-finite values.
Results may differ from a plain program's by a relative error of at most 0.006.
Values may be sent and summed in bfloat16 or wider, within the bound.
No kernel may reach another device: no remote copies, remote signals or barrier semaphores. Data moves between devices by JAX's collectives and lax.ppermute only.
A program may use at most 64 MiB of HBM per device.

v0:
```python
import math

import jax
import jax.numpy as jnp
from jax import lax
from jax.experimental import pallas as pl
from jax.experimental.pallas import tpu as pltpu
from jax.sharding import Mesh
from jax.sharding import PartitionSpec as P


AXES = ("X", "ZH", "ZL", "Y", "C")
DOM = ("X", "ZH", "ZL")
REP = ("Y", "C")
N_X, N_Z, FOUR = 4, 16, 4

SECOND = (((0, 2), (2, 1), (2, -1)), ((2, 0), (1, 2), (-1, -2)))
THIRD = (((1, 0), (-1, 0), (0, 1), (0, -1)), ((0, 1), (0, -1), (1, 0), (-1, 0)))
PIECES = (16, 16, 16, 8, 8)
BLK = 128


def place_table(core):
    held = ((0, 0),) + SECOND[core]
    table = {k: 4 * i for i, k in enumerate(held)}
    at = PIECES[0]
    for i, (dx, dz) in enumerate(THIRD[core]):
        sent = held if i < 2 else (held[0], held[2])
        for hx, hz in sent:
            table[(hx + dx, hz + dz)] = at
            at += 4
    flat = [None] * (N_X * FOUR)
    for (dx, dl), start in table.items():
        flat[dx % N_X * FOUR + dl % FOUR] = start
    return flat


def shift(value, first, second):
    pairs = []
    for x in range(N_X):
        for z in range(N_Z):
            for core, (dx, dz) in enumerate((first, second)):
                if (dx, dz) == (0, 2) and z % 2:
                    dz = -2
                source = (x + dx) % N_X * N_Z + (z + dz) % N_Z
                pairs.append((source * 2 + core, (x * N_Z + z) * 2 + core))
    return lax.ppermute(value, DOM + ("C",), pairs)


def halves(value):
    high = lax.reduce_precision(value, 8, 7)
    low = lax.reduce_precision(value - high, 8, 7)
    return jnp.concatenate([high, low], axis=-2).astype(jnp.bfloat16)


def whole(pair):
    high, low = jnp.split(pair.astype(jnp.float32), 2, axis=-2)
    return high + low


def gather_panels(value, riding=None):
    rows, width = value.shape

    def stacked(parts, pair):
        return jnp.concatenate(parts if pair is None else [*parts, pair], axis=0)

    got = lax.all_gather(stacked([value], riding), "ZH", axis=0, tiled=False)
    own = got[:, :rows].reshape(-1, width)
    size, pair = own.shape[0], None
    if riding is not None:
        pair = halves(jnp.sum(got[:, rows:].astype(jnp.float32), axis=0))
    packed = stacked([own], pair)
    more = []
    for steps in zip(*SECOND):
        more.append(shift(packed, *steps))
    if riding is not None:
        terms = [whole(pair)]
        for m in more:
            terms.append(whole(m[size:]))
        pair = halves((terms[0] + terms[1]) + (terms[2] + terms[3]))
    held = stacked([own] + [m[:size] for m in more], pair)
    half = jnp.concatenate(lax.optimization_barrier([own, more[1][:size]]), axis=0)
    near = []
    for i, steps in enumerate(zip(*THIRD)):
        sent = held if i < 2 else half if i == 2 else stacked([half], pair)
        near.append(shift(sent, *steps))
    total = None
    if riding is not None:
        n = pair.shape[0]
        plus, minus, side = (whole(near[i][-n:]) for i in (0, 1, 3))
        total = (whole(pair) + side) + (plus + minus)
    return (held, *near), total


def places(columns):
    cols = columns.T
    dx = (cols // N_Z - lax.axis_index("X")) % N_X
    dl = (cols - lax.axis_index("ZL")) % FOUR
    kind = dx * FOUR + dl
    core = lax.axis_index("C")
    base = jnp.zeros_like(cols)
    for k, (zero, one) in enumerate(zip(place_table(0), place_table(1))):
        base = jnp.where(kind == k, jnp.where(core == 0, zero, one), base)
    return (base + cols // FOUR % FOUR) * BLK


def product_kernel(place_ref, values_ref, *refs):
    pieces, (out_ref, panels, blocks, piece_sem, block_sem) = refs[:5], refs[5:]
    rows, rounds, blk, _ = blocks.shape
    copies = []
    for a in range(rows):
        copies.append(pltpu.make_async_copy(values_ref.at[:, a], blocks.at[a], block_sem.at[a]))
    moves, at = [], 0
    for i, piece in enumerate(pieces):
        n = PIECES[i] * blk
        moves.append(
            pltpu.make_async_copy(
                piece.at[pl.ds(0, n)], panels.at[pl.ds(at, n)], piece_sem.at[i]
            )
        )
        at += n
    for move in moves:
        move.start()
    for copy in copies:
        copy.start()
    for move in moves:
        move.wait()

    def panel(a, t):
        return panels[pl.ds(pl.multiple_of(place_ref[a, t], blk), blk)]

    for a in range(rows):
        copies[a].wait()
        total = None
        for t in range(0, rounds, 2):
            left = jnp.concatenate([blocks[a, t], blocks[a, t + 1]], axis=1)
            right = jnp.concatenate([panel(a, t), panel(a, t + 1)], axis=0)
            term = jnp.dot(left, right, preferred_element_type=jnp.float32)
            total = term if total is None else total + term
        out_ref[a, 0:blk] = total.astype(out_ref.dtype)


def panel_products(values, place, pieces, spare=0):
    rounds, rows, blk, _ = values.shape
    width = pieces[0].shape[-1]
    any_space = pl.BlockSpec(memory_space=pl.ANY)
    return pl.pallas_call(
        product_kernel,
        out_shape=jax.ShapeDtypeStruct((rows, blk + spare, width), jnp.bfloat16),
        in_specs=[
            pl.BlockSpec(memory_space=pltpu.SMEM),
            any_space,
        ]
        + [any_space] * 5,
        out_specs=pl.BlockSpec(memory_space=pltpu.VMEM),
        scratch_shapes=[
            pltpu.VMEM((sum(PIECES) * blk, width), jnp.bfloat16),
            pltpu.VMEM((rows, rounds, blk, blk), jnp.bfloat16),
            pltpu.SemaphoreType.DMA((5,)),
            pltpu.SemaphoreType.DMA((rows,)),
        ],
        compiler_params=pltpu.CompilerParams(vmem_limit_bytes=24 * 2**20),
        cost_estimate=pl.CostEstimate(
            flops=2 * rounds * rows * blk * blk * width, bytes_accessed=9 * 2**20, transcendentals=0
        ),
        name="panel_products",
    )(place, values, *pieces)


def summed_over_rep(partial):
    received = lax.all_to_all(partial, REP, 0, 0, tiled=True)
    return jnp.sum(received.astype(jnp.float32), axis=0)


def dense_grads(hidden, weight, cotangent):
    pre_act = jnp.dot(hidden, weight, preferred_element_type=jnp.float32)
    sigmoid_value = jax.nn.sigmoid(pre_act)
    slope_value = sigmoid_value * (1.0 + pre_act * (1.0 - sigmoid_value))
    grad_pre = (cotangent.astype(jnp.float32) * slope_value).astype(jnp.bfloat16)
    hidden_grad = jnp.einsum(
        "rg,fg->rf", grad_pre, weight, preferred_element_type=jnp.float32
    ).astype(jnp.bfloat16)
    weight_part = jnp.einsum("rf,rg->fg", hidden, grad_pre, preferred_element_type=jnp.float32)
    return hidden_grad, weight_part


def shards(features, block_values, block_columns, weight, cotangent):
    values = block_values[0]
    rows, f = features.shape
    node_total = rows * lax.axis_size(AXES)
    inv_scale = 1.0 / math.sqrt(node_total)
    place = places(block_columns[0])
    panels, _ = gather_panels(features)
    partial = panel_products(pltpu.with_memory_space_constraint(values, pltpu.HBM), place, panels)
    hidden = summed_over_rep(partial).astype(jnp.bfloat16)
    hidden_grad, weight_part = dense_grads(hidden, weight, cotangent)
    n_rep = lax.axis_size(REP)
    slices = lax.all_to_all(weight_part.reshape(n_rep, -1, f), REP, 0, 0, tiled=True)
    weight_slice = jnp.sum(slices, axis=0).astype(jnp.bfloat16)
    panels, weight_slice = gather_panels(hidden_grad, weight_slice)
    extra = weight_slice.shape[0]
    back = panel_products(values, place, panels, extra)
    back = back.at[:, rows:].set(weight_slice.astype(jnp.bfloat16)[None])
    received = lax.all_to_all(back, REP, 0, 0, tiled=True).astype(jnp.float32)
    feature_grad = jnp.sum(received[:, :rows], axis=0).astype(jnp.bfloat16)
    weight_grad = received[:, rows:].reshape(f, f) * inv_scale
    return feature_grad, weight_grad


def solution(mesh):
    finer = Mesh(mesh.devices.reshape(4, 4, 4, 4, 2), AXES)
    in_specs = (
        P(AXES, None),
        P(AXES, None, None, None, None),
        P(AXES, None, None),
        P(),
        P(AXES, None),
    )
    out_specs = (P(AXES, None), P())
    return jax.shard_map(
        shards, mesh=finer, in_specs=in_specs, out_specs=out_specs, check_vma=False
    )
```

profile of v0, /device:TPU:1, one launch (start us, length us, event | category | flops | bytes accessed | tf_op | source)
XLA Modules:
  0.0 200.3 jit_solution(16680730972310076085)
XLA Ops:
  0.6 0.0 copy-start
  0.6 25.6 %all-gather = bf16[512,256]{1,0:T(8,128)(2,1)S(1)} all-gather(bf16[128,256]{1,0:T(8,128)(2,1)} %param.7), channel_id=2, replica_groups=mesh['X'=4,'ZH'=4,'ZL'=4,'Y'=4,'C'=2] {'ZH'}, dimensions={0}, use_global_device_ids=true | all-gather | bytes 327680 | tf_op jit(solution)/shard_map/all_gather | solution.py:67
  26.2 4.6 %collective-permute-start = (bf16[512,256]{1,0:T(8,128)(2,1)S(1)}, bf16[512,256]{1,0:T(8,128)(2,1)S(1)}, u32[]{:S(2)}, u32[]{:S(2)}) collective-permute-start(bf16[512,256]{1,0:T(8,128)(2,1)S(1)} %all-gather), channel_id=1, source_target_pairs={{16,0},{257,1},{120,8},{265,9},{32,16},{273,17},{8,24},{281,25},{4... | collective-permute-start | bytes 786440 | tf_op jit(solution)/shard_map/ppermute | solution.py:47
  30.9 3.3 %collective-permute-start.1 = (bf16[512,256]{1,0:T(8,128)(2,1)S(1)}, bf16[512,256]{1,0:T(8,128)(2,1)S(1)}, u32[]{:S(2)}, u32[]{:S(2)}) collective-permute-start(bf16[512,256]{1,0:T(8,128)(2,1)S(1)} %all-gather), channel_id=1, source_target_pairs={{264,0},{145,1},{272,8},{153,9},{280,16},{161,17},{288,24},{169,25... | collective-permute-start | bytes 786440 | tf_op jit(solution)/shard_map/ppermute | solution.py:47
  34.2 3.8 %collective-permute-start.2 = (bf16[512,256]{1,0:T(8,128)(2,1)S(1)}, bf16[512,256]{1,0:T(8,128)(2,1)S(1)}, u32[]{:S(2)}, u32[]{:S(2)}) collective-permute-start(bf16[512,256]{1,0:T(8,128)(2,1)S(1)} %all-gather), channel_id=1, source_target_pairs={{376,0},{497,1},{256,8},{505,9},{264,16},{385,17},{272,24},{393,25... | collective-permute-start | bytes 786440 | tf_op jit(solution)/shard_map/ppermute | solution.py:47
  38.0 0.0 collective-permute-done
  38.0 0.0 copy-start.2
  38.1 6.7 %collective-permute-done.1 = bf16[512,256]{1,0:T(8,128)(2,1)S(1)} collective-permute-done((bf16[512,256]{1,0:T(8,128)(2,1)S(1)}, bf16[512,256]{1,0:T(8,128)(2,1)S(1)}, u32[]{:S(2)}, u32[]{:S(2)}) %collective-permute-start.1) | collective-permute-done | bytes 262176 | tf_op jit(solution)/shard_map/ppermute | solution.py:47
  44.8 2.8 %collective-permute-done.2 = bf16[512,256]{1,0:T(8,128)(2,1)S(1)} collective-permute-done((bf16[512,256]{1,0:T(8,128)(2,1)S(1)}, bf16[512,256]{1,0:T(8,128)(2,1)S(1)}, u32[]{:S(2)}, u32[]{:S(2)}) %collective-permute-start.2) | collective-permute-done | bytes 262176 | tf_op jit(solution)/shard_map/ppermute | solution.py:47
  47.6 4.8 %collective-permute-start.3 = (bf16[2048,256]{1,0:T(8,128)(2,1)S(1)}, bf16[2048,256]{1,0:T(8,128)(2,1)S(1)}, u32[]{:S(2)}, u32[]{:S(2)}) collective-permute-start(bf16[2048,256]{1,0:T(8,128)(2,1)S(1)} %constant_dynamic-update-slice_fusion.refs_0_), channel_id=1, source_target_pairs={{128,0},{9,1},{136,8},{17,9},{144,16},{25,17},{152,24},{33,25},{16... | collective-permute-start | bytes 3145736 | tf_op jit(solution)/shard_map/ppermute | solution.py:47
  52.4 4.9 %collective-permute-start.4 = (bf16[2048,256]{1,0:T(8,128)(2,1)S(1)}, bf16[2048,256]{1,0:T(8,128)(2,1)S(1)}, u32[]{:S(2)}, u32[]{:S(2)}) collective-permute-start(bf16[2048,256]{1,0:T(8,128)(2,1)S(1)} %constant_dynamic-update-slice_fusion.refs_0_), channel_id=1, source_target_pairs={{384,0},{121,1},{392,8},{1,9},{400,16},{9,17},{408,24},{17,25},{41... | collective-permute-start | bytes 3145736 | tf_op jit(solution)/shard_map/ppermute | solution.py:47
  57.3 0.7 constant_dynamic-update-slice_fusion.5
  58.0 0.7 constant_dynamic-update-slice_fusion.4
  58.8 1.9 collective-permute-start.5
  60.7 3.4 %collective-permute-start.6 = (bf16[1024,256]{1,0:T(8,128)(2,1)}, bf16[1024,256]{1,0:T(8,128)(2,1)}, u32[]{:S(2)}, u32[]{:S(2)}) collective-permute-start(bf16[1024,256]{1,0:T(8,128)(2,1)} %constant_dynamic-update-slice_fusion.4), channel_id=1, source_target_pairs={{120,0},{385,1},{0,8},{393,9},{8,16},{401,17},{16,24},{409,25},{24... | collective-permute-start | bytes 1572872 | tf_op jit(solution)/shard_map/ppermute | solution.py:47
  64.1 0.0 copy-done.2
  64.1 10.8 %collective-permute-done.5.refs_3_ = bf16[1024,256]{1,0:T(8,128)(2,1)} collective-permute-done((bf16[1024,256]{1,0:T(8,128)(2,1)}, bf16[1024,256]{1,0:T(8,128)(2,1)}, u32[]{:S(2)}, u32[]{:S(2)}) %collective-permute-start.5) | collective-permute-done | bytes 524320 | tf_op jit(solution)/shard_map/ppermute | solution.py:47
  74.9 3.0 %collective-permute-done.6.refs_4_ = bf16[1024,256]{1,0:T(8,128)(2,1)} collective-permute-done((bf16[1024,256]{1,0:T(8,128)(2,1)}, bf16[1024,256]{1,0:T(8,128)(2,1)}, u32[]{:S(2)}, u32[]{:S(2)}) %collective-permute-start.6) | collective-permute-done | bytes 524320 | tf_op jit(solution)/shard_map/ppermute | solution.py:47
  77.9 0.0 collective-permute-done.3.refs_1_
  77.9 0.0 collective-permute-done.4.refs_2_
  77.9 6.6 %panel_products.2 = bf16[8,128,256]{2,1,0:T(8,128)(2,1)S(1)} custom-call(s32[8,16]{1,0:T(8,128)S(1)} %fusion.22.place_ref, bf16[16,8,128,128]{3,2,1,0:T(8,128)(2,1)} %bitcast.44, bf16[2048,256]{1,0:T(8,128)(2,1)S(1)} %constant_dynamic-update-slice_fusion.refs_0_, bf16[2048,256]{1,0:T(8,128)(2,1)S(1)} %collective-permute-done.3.refs_1_, ...), custom_call_target="tpu_custom_call" | custom-call | flops 1073741824 | bytes 9437184 | tf_op jit(solution)/shard_map/panel_products/pallas_call | solution.py:147
  84.6 0.0 copy-start.3
  84.6 14.5 %all_to_all.15 = bf16[8,128,256]{2,1,0:T(8,128)(2,1)S(1)} all-to-all(bf16[8,128,256]{2,1,0:T(8,128)(2,1)S(1)} %panel_products.2), channel_id=1, replica_groups=mesh['X'=4,'ZH'=4,'ZL'=4,'Y'=4,'C'=2] {'Y','C'}, dimensions={0} | all-to-all | bytes 1048576 | tf_op jit(solution)/shard_map/all_to_all | solution.py:171
  99.1 0.1 reduce_sum.39
  99.2 0.0 copy-done
  99.2 0.2 fusion.30
  99.3 0.1 copy.8
  99.5 0.0 copy-done.3
  99.5 0.9 fusion
  100.4 4.4 %all-to-all-start.1 = ((f32[8,32,256]{2,1,0:T(8,128)}), f32[8,32,256]{2,1,0:T(8,128)S(1)}, u32[]{:S(2)}, u32[]{:S(2)}) async-start(f32[8,32,256]{2,1,0:T(8,128)} %fusion), calls=%async_computation.1 | async-start | bytes 524288 | tf_op jit(solution)/shard_map/all_to_all | solution.py:198
  104.7 0.2 convolution_convert_fusion
  104.9 6.3 %all-to-all-done.1 = f32[8,32,256]{2,1,0:T(8,128)S(1)} async-done(((f32[8,32,256]{2,1,0:T(8,128)}), f32[8,32,256]{2,1,0:T(8,128)S(1)}, u32[]{:S(2)}, u32[]{:S(2)}) %all-to-all-start.1) | async-done | bytes 262176 | tf_op jit(solution)/shard_map/all_to_all | solution.py:198
  111.3 16.5 %all-gather.1 = bf16[640,256]{1,0:T(8,128)(2,1)S(1)} all-gather(bf16[160,256]{1,0:T(8,128)(2,1)S(1)} %pad_maximum_fusion.3), channel_id=3, replica_groups=mesh['X'=4,'ZH'=4,'ZL'=4,'Y'=4,'C'=2] {'ZH'}, dimensions={0}, use_global_device_ids=true | all-gather | bytes 409600 | tf_op jit(solution)/shard_map/all_gather | solution.py:67
  127.9 3.1 %collective-permute-start.7 = (bf16[576,256]{1,0:T(8,128)(2,1)S(1)}, bf16[576,256]{1,0:T(8,128)(2,1)S(1)}, u32[]{:S(2)}, u32[]{:S(2)}) collective-permute-start(bf16[576,256]{1,0:T(8,128)(2,1)S(1)} %pad_maximum_fusion.2), channel_id=1, source_target_pairs={{16,0},{257,1},{120,8},{265,9},{32,16},{273,17},{8,24},{281,25},{4... | collective-permute-start | bytes 884744 | tf_op jit(solution)/shard_map/ppermute | solution.py:47
  131.0 5.2 %collective-permute-start.8 = (bf16[576,256]{1,0:T(8,128)(2,1)S(1)}, bf16[576,256]{1,0:T(8,128)(2,1)S(1)}, u32[]{:S(2)}, u32[]{:S(2)}) collective-permute-start(bf16[576,256]{1,0:T(8,128)(2,1)S(1)} %pad_maximum_fusion.2), channel_id=1, source_target_pairs={{264,0},{145,1},{272,8},{153,9},{280,16},{161,17},{288,24},{169,25... | collective-permute-start | bytes 884744 | tf_op jit(solution)/shard_map/ppermute | solution.py:47
  136.2 1.9 collective-permute-start.9
  138.2 0.0 collective-permute-done.7
  138.2 4.3 %collective-permute-done.8 = bf16[576,256]{1,0:T(8,128)(2,1)S(1)} collective-permute-done((bf16[576,256]{1,0:T(8,128)(2,1)S(1)}, bf16[576,256]{1,0:T(8,128)(2,1)S(1)}, u32[]{:S(2)}, u32[]{:S(2)}) %collective-permute-start.8) | collective-permute-done | bytes 294944 | tf_op jit(solution)/shard_map/ppermute | solution.py:47
  142.5 0.0 copy-start.1
  142.6 6.9 %collective-permute-done.9 = bf16[576,256]{1,0:T(8,128)(2,1)S(1)} collective-permute-done((bf16[576,256]{1,0:T(8,128)(2,1)S(1)}, bf16[576,256]{1,0:T(8,128)(2,1)S(1)}, u32[]{:S(2)}, u32[]{:S(2)}) %collective-permute-start.9) | collective-permute-done | bytes 294944 | tf_op jit(solution)/shard_map/ppermute | solution.py:47
  149.6 7.6 %collective-permute-start.11 = (bf16[2112,256]{1,0:T(8,128)(2,1)S(1)}, bf16[2112,256]{1,0:T(8,128)(2,1)S(1)}, u32[]{:S(2)}, u32[]{:S(2)}) collective-permute-start(bf16[2112,256]{1,0:T(8,128)(2,1)S(1)} %get-tuple-element.22.refs_0_), channel_id=1, source_target_pairs={{384,0},{121,1},{392,8},{1,9},{400,16},{9,17},{408,24},{17,25},{41... | collective-permute-start | bytes 3244040 | tf_op jit(solution)/shard_map/ppermute | solution.py:47
  157.1 3.5 %collective-permute-start.10 = (bf16[2112,256]{1,0:T(8,128)(2,1)S(1)}, bf16[2112,256]{1,0:T(8,128)(2,1)S(1)}, u32[]{:S(2)}, u32[]{:S(2)}) collective-permute-start(bf16[2112,256]{1,0:T(8,128)(2,1)S(1)} %get-tuple-element.22.refs_0_), channel_id=1, source_target_pairs={{128,0},{9,1},{136,8},{17,9},{144,16},{25,17},{152,24},{33,25},{16... | collective-permute-start | bytes 3244040 | tf_op jit(solution)/shard_map/ppermute | solution.py:47
  160.6 1.9 collective-permute-start.13
  162.6 4.6 %collective-permute-start.12 = (bf16[1024,256]{1,0:T(8,128)(2,1)S(1)}, bf16[1024,256]{1,0:T(8,128)(2,1)S(1)}, u32[]{:S(2)}, u32[]{:S(2)}) collective-permute-start(bf16[1024,256]{1,0:T(8,128)(2,1)S(1)} %pad_maximum_fusion.1), channel_id=1, source_target_pairs={{8,0},{129,1},{16,8},{137,9},{24,16},{145,17},{32,24},{153,25},{40... | collective-permute-start | bytes 1572872 | tf_op jit(solution)/shard_map/ppermute | solution.py:47
  167.2 11.2 %collective-permute-done.13.refs_4_ = bf16[1088,256]{1,0:T(8,128)(2,1)S(1)} collective-permute-done((bf16[1088,256]{1,0:T(8,128)(2,1)S(1)}, bf16[1088,256]{1,0:T(8,128)(2,1)S(1)}, u32[]{:S(2)}, u32[]{:S(2)}) %collective-permute-start.13) | collective-permute-done | bytes 557088 | tf_op jit(solution)/shard_map/ppermute | solution.py:47
  178.4 0.0 collective-permute-done.11.refs_2_
  178.4 0.0 collective-permute-done.10.refs_1_
  178.5 0.4 collective-permute-done.12.refs_3_
  178.9 0.0 copy-done.1
  178.9 4.7 %panel_products.3 = bf16[8,160,256]{2,1,0:T(8,128)(2,1)S(1)} custom-call(s32[8,16]{1,0:T(8,128)S(1)} %fusion.22.place_ref, bf16[16,8,128,128]{3,2,1,0:T(8,128)(2,1)S(1)} %bitcast.45, bf16[2112,256]{1,0:T(8,128)(2,1)S(1)} %get-tuple-element.22.refs_0_, bf16[2112,256]{1,0:T(8,128)(2,1)S(1)} %collective-permute-done.10.refs_1_, ...), custom_call_target="tpu_custom_call" | custom-call | flops 1073741824 | bytes 9437184 | tf_op jit(solution)/shard_map/panel_products/pallas_call | solution.py:147
  183.6 15.2 %all_to_all.16 = bf16[8,160,256]{2,1,0:T(8,128)(2,1)S(1)} all-to-all(bf16[8,160,256]{2,1,0:T(8,128)(2,1)S(1)} %broadcast_dynamic-update-slice_fusion), channel_id=1, replica_groups=mesh['X'=4,'ZH'=4,'ZL'=4,'Y'=4,'C'=2] {'Y','C'}, dimensions={0} | all-to-all | bytes 1310720 | tf_op jit(solution)/shard_map/all_to_all | solution.py:204
  198.8 0.1 convert_element_type.66
  198.9 0.7 slice_multiply_fusion
  199.6 0.7 slice_reduce_fusion
  (29 shorter events, 0.5 us)
Async XLA Ops:
  0.6 98.5 %copy-start = (bf16[256,256]{1,0:T(8,128)(2,1)S(1)}, bf16[256,256]{1,0:T(8,128)(2,1)}, u32[]{:S(2)}) copy-start(bf16[256,256]{1,0:T(8,128)(2,1)} %param.10) | copy-start | bytes 393220
  26.2 11.8 %collective-permute-start = (bf16[512,256]{1,0:T(8,128)(2,1)S(1)}, bf16[512,256]{1,0:T(8,128)(2,1)S(1)}, u32[]{:S(2)}, u32[]{:S(2)}) collective-permute-start(bf16[512,256]{1,0:T(8,128)(2,1)S(1)} %all-gather), channel_id=1, source_target_pairs={{16,0},{257,1},{120,8},{265,9},{32,16},{273,17},{8,24},{281,25},{4... | collective-permute-start | bytes 786440 | tf_op jit(solution)/shard_map/ppermute | solution.py:47
  30.9 13.9 %collective-permute-start.1 = (bf16[512,256]{1,0:T(8,128)(2,1)S(1)}, bf16[512,256]{1,0:T(8,128)(2,1)S(1)}, u32[]{:S(2)}, u32[]{:S(2)}) collective-permute-start(bf16[512,256]{1,0:T(8,128)(2,1)S(1)} %all-gather), channel_id=1, source_target_pairs={{264,0},{145,1},{272,8},{153,9},{280,16},{161,17},{288,24},{169,25... | collective-permute-start | bytes 786440 | tf_op jit(solution)/shard_map/ppermute | solution.py:47
  34.2 13.4 %collective-permute-start.2 = (bf16[512,256]{1,0:T(8,128)(2,1)S(1)}, bf16[512,256]{1,0:T(8,128)(2,1)S(1)}, u32[]{:S(2)}, u32[]{:S(2)}) collective-permute-start(bf16[512,256]{1,0:T(8,128)(2,1)S(1)} %all-gather), channel_id=1, source_target_pairs={{376,0},{497,1},{256,8},{505,9},{264,16},{385,17},{272,24},{393,25... | collective-permute-start | bytes 786440 | tf_op jit(solution)/shard_map/ppermute | solution.py:47
  38.0 26.0 %copy-start.2 = (s32[1,16,8]{1,2,0:T(8,128)S(1)}, s32[1,16,8]{1,2,0:T(8,128)}, u32[]{:S(2)}) copy-start(s32[1,16,8]{1,2,0:T(8,128)} %param.9) | copy-start | bytes 1540
  47.6 30.4 %collective-permute-start.3 = (bf16[2048,256]{1,0:T(8,128)(2,1)S(1)}, bf16[2048,256]{1,0:T(8,128)(2,1)S(1)}, u32[]{:S(2)}, u32[]{:S(2)}) collective-permute-start(bf16[2048,256]{1,0:T(8,128)(2,1)S(1)} %constant_dynamic-update-slice_fusion.refs_0_), channel_id=1, source_target_pairs={{128,0},{9,1},{136,8},{17,9},{144,16},{25,17},{152,24},{33,25},{16... | collective-permute-start | bytes 3145736 | tf_op jit(solution)/shard_map/ppermute | solution.py:47
  52.4 25.5 %collective-permute-start.4 = (bf16[2048,256]{1,0:T(8,128)(2,1)S(1)}, bf16[2048,256]{1,0:T(8,128)(2,1)S(1)}, u32[]{:S(2)}, u32[]{:S(2)}) collective-permute-start(bf16[2048,256]{1,0:T(8,128)(2,1)S(1)} %constant_dynamic-update-slice_fusion.refs_0_), channel_id=1, source_target_pairs={{384,0},{121,1},{392,8},{1,9},{400,16},{9,17},{408,24},{17,25},{41... | collective-permute-start | bytes 3145736 | tf_op jit(solution)/shard_map/ppermute | solution.py:47
  58.8 16.1 %collective-permute-start.5 = (bf16[1024,256]{1,0:T(8,128)(2,1)}, bf16[1024,256]{1,0:T(8,128)(2,1)}, u32[]{:S(2)}, u32[]{:S(2)}) collective-permute-start(bf16[1024,256]{1,0:T(8,128)(2,1)} %constant_dynamic-update-slice_fusion.4), channel_id=1, source_target_pairs={{8,0},{129,1},{16,8},{137,9},{24,16},{145,17},{32,24},{153,25},{40... | collective-permute-start | bytes 1572872 | tf_op jit(solution)/shard_map/ppermute | solution.py:47
  60.7 17.3 %collective-permute-start.6 = (bf16[1024,256]{1,0:T(8,128)(2,1)}, bf16[1024,256]{1,0:T(8,128)(2,1)}, u32[]{:S(2)}, u32[]{:S(2)}) collective-permute-start(bf16[1024,256]{1,0:T(8,128)(2,1)} %constant_dynamic-update-slice_fusion.4), channel_id=1, source_target_pairs={{120,0},{385,1},{0,8},{393,9},{8,16},{401,17},{16,24},{409,25},{24... | collective-permute-start | bytes 1572872 | tf_op jit(solution)/shard_map/ppermute | solution.py:47
  84.6 14.9 %copy-start.3 = (bf16[128,256]{1,0:T(8,128)(2,1)S(1)}, bf16[128,256]{1,0:T(8,128)(2,1)}, u32[]{:S(2)}) copy-start(bf16[128,256]{1,0:T(8,128)(2,1)} %param.11) | copy-start | bytes 196612
  100.4 10.9 %all-to-all-start.1 = ((f32[8,32,256]{2,1,0:T(8,128)}), f32[8,32,256]{2,1,0:T(8,128)S(1)}, u32[]{:S(2)}, u32[]{:S(2)}) async-start(f32[8,32,256]{2,1,0:T(8,128)} %fusion), calls=%async_computation.1 | async-start | bytes 524288 | tf_op jit(solution)/shard_map/all_to_all | solution.py:198
  127.9 10.3 %collective-permute-start.7 = (bf16[576,256]{1,0:T(8,128)(2,1)S(1)}, bf16[576,256]{1,0:T(8,128)(2,1)S(1)}, u32[]{:S(2)}, u32[]{:S(2)}) collective-permute-start(bf16[576,256]{1,0:T(8,128)(2,1)S(1)} %pad_maximum_fusion.2), channel_id=1, source_target_pairs={{16,0},{257,1},{120,8},{265,9},{32,16},{273,17},{8,24},{281,25},{4... | collective-permute-start | bytes 884744 | tf_op jit(solution)/shard_map/ppermute | solution.py:47
  131.0 11.6 %collective-permute-start.8 = (bf16[576,256]{1,0:T(8,128)(2,1)S(1)}, bf16[576,256]{1,0:T(8,128)(2,1)S(1)}, u32[]{:S(2)}, u32[]{:S(2)}) collective-permute-start(bf16[576,256]{1,0:T(8,128)(2,1)S(1)} %pad_maximum_fusion.2), channel_id=1, source_target_pairs={{264,0},{145,1},{272,8},{153,9},{280,16},{161,17},{288,24},{169,25... | collective-permute-start | bytes 884744 | tf_op jit(solution)/shard_map/ppermute | solution.py:47
  136.2 13.3 %collective-permute-start.9 = (bf16[576,256]{1,0:T(8,128)(2,1)S(1)}, bf16[576,256]{1,0:T(8,128)(2,1)S(1)}, u32[]{:S(2)}, u32[]{:S(2)}) collective-permute-start(bf16[576,256]{1,0:T(8,128)(2,1)S(1)} %pad_maximum_fusion.2), channel_id=1, source_target_pairs={{376,0},{497,1},{256,8},{505,9},{264,16},{385,17},{272,24},{393,25... | collective-permute-start | bytes 884744 | tf_op jit(solution)/shard_map/ppermute | solution.py:47
  142.5 36.4 %copy-start.1 = (bf16[1,16,8,128,128]{4,3,2,1,0:T(8,128)(2,1)S(1)}, bf16[1,16,8,128,128]{4,3,2,1,0:T(8,128)(2,1)}, u32[]{:S(2)}) copy-start(bf16[1,16,8,128,128]{4,3,2,1,0:T(8,128)(2,1)} %param.8) | copy-start | bytes 12582916
  149.6 28.8 %collective-permute-start.11 = (bf16[2112,256]{1,0:T(8,128)(2,1)S(1)}, bf16[2112,256]{1,0:T(8,128)(2,1)S(1)}, u32[]{:S(2)}, u32[]{:S(2)}) collective-permute-start(bf16[2112,256]{1,0:T(8,128)(2,1)S(1)} %get-tuple-element.22.refs_0_), channel_id=1, source_target_pairs={{384,0},{121,1},{392,8},{1,9},{400,16},{9,17},{408,24},{17,25},{41... | collective-permute-start | bytes 3244040 | tf_op jit(solution)/shard_map/ppermute | solution.py:47
  157.1 21.3 %collective-permute-start.10 = (bf16[2112,256]{1,0:T(8,128)(2,1)S(1)}, bf16[2112,256]{1,0:T(8,128)(2,1)S(1)}, u32[]{:S(2)}, u32[]{:S(2)}) collective-permute-start(bf16[2112,256]{1,0:T(8,128)(2,1)S(1)} %get-tuple-element.22.refs_0_), channel_id=1, source_target_pairs={{128,0},{9,1},{136,8},{17,9},{144,16},{25,17},{152,24},{33,25},{16... | collective-permute-start | bytes 3244040 | tf_op jit(solution)/shard_map/ppermute | solution.py:47
  160.6 17.8 %collective-permute-start.13 = (bf16[1088,256]{1,0:T(8,128)(2,1)S(1)}, bf16[1088,256]{1,0:T(8,128)(2,1)S(1)}, u32[]{:S(2)}, u32[]{:S(2)}) collective-permute-start(bf16[1088,256]{1,0:T(8,128)(2,1)S(1)} %pad_maximum_fusion), channel_id=1, source_target_pairs={{120,0},{385,1},{0,8},{393,9},{8,16},{401,17},{16,24},{409,25},{24... | collective-permute-start | bytes 1671176 | tf_op jit(solution)/shard_map/ppermute | solution.py:47
  162.6 16.3 %collective-permute-start.12 = (bf16[1024,256]{1,0:T(8,128)(2,1)S(1)}, bf16[1024,256]{1,0:T(8,128)(2,1)S(1)}, u32[]{:S(2)}, u32[]{:S(2)}) collective-permute-start(bf16[1024,256]{1,0:T(8,128)(2,1)S(1)} %pad_maximum_fusion.1), channel_id=1, source_target_pairs={{8,0},{129,1},{16,8},{137,9},{24,16},{145,17},{32,24},{153,25},{40... | collective-permute-start | bytes 1572872 | tf_op jit(solution)/shard_map/ppermute | solution.py:47
where the time goes:
time: 201 us; the launch traced here: 200 us
  blocking collectives  71.7 us (36%)
  starting transfers between devices  58.8 us (29%)
  waiting for transfers between devices  52.4 us (26%)
  Pallas kernels  11.3 us (6%)
    ppermute x14, starting transfers between devices, shift(): return lax.ppermute(value, DOM + ('C',), pairs)  54.5 us
    ppermute x14, waiting for transfers between devices, shift(): return lax.ppermute(value, DOM + ('C',), pairs)  46.1 us
    all_gather x2, blocking collectives, gather_panels(): got = lax.all_gather(stacked([value], riding), 'ZH', axis=0, tiled=False)  42.1 us
    all_to_all x1, blocking collectives, shards(): received = lax.all_to_all(back, REP, 0, 0, tiled=True).astype(jnp.float32)  15.2 us
    all_to_all x1, blocking collectives, summed_over_rep(): received = lax.all_to_all(partial, REP, 0, 0, tiled=True)  14.5 us
    pallas_call x2, Pallas kernels, panel_products(): pl.pallas_call(product_kernel, out_shape=jax.ShapeDtypeStruct((rows, blk...  11.3 us
    all_to_all x1, waiting for transfers between devices, shards(): lax.all_to_all(weight_part.reshape(n_rep, -1, f), REP, 0, 0, tiled=True)  6.3 us
    all_to_all x1, starting transfers between devices, shards(): lax.all_to_all(weight_part.reshape(n_rep, -1, f), REP, 0, 0, tiled=True)  4.36 us
  transfers between devices with their start and end apart: 15, of which 9 were waited for; matrix products, arithmetic and copies ran while one was open for 1% of the time, Pallas kernels for 0%

commit v1 on v0

--- a/solution.py
+++ b/solution.py
@@ -104,12 +104,27 @@
     return (base + cols // FOUR % FOUR) * BLK
 
 
+def load_kernel(values_ref, out_ref, sem):
+    copy = pltpu.make_async_copy(values_ref, out_ref, sem)
+    copy.start()
+    copy.wait()
+
+
+def loaded(values):
+    return pl.pallas_call(
+        load_kernel,
+        out_shape=jax.ShapeDtypeStruct(values.shape, values.dtype),
+        in_specs=[pl.BlockSpec(memory_space=pl.ANY)],
+        out_specs=pl.BlockSpec(memory_space=pltpu.VMEM),
+        scratch_shapes=[pltpu.SemaphoreType.DMA],
+        compiler_params=pltpu.CompilerParams(vmem_limit_bytes=2**20),
+        name="load_blocks",
+    )(pltpu.with_memory_space_constraint(values, pltpu.HBM))
+
+
 def product_kernel(place_ref, values_ref, *refs):
-    pieces, (out_ref, panels, blocks, piece_sem, block_sem) = refs[:5], refs[5:]
-    rows, rounds, blk, _ = blocks.shape
-    copies = []
-    for a in range(rows):
-        copies.append(pltpu.make_async_copy(values_ref.at[:, a], blocks.at[a], block_sem.at[a]))
+    pieces, (out_ref, panels, piece_sem) = refs[:5], refs[5:]
+    rounds, rows, blk, _ = values_ref.shape
     moves, at = [], 0
     for i, piece in enumerate(pieces):
         n = PIECES[i] * blk
@@ -121,8 +136,6 @@
         at += n
     for move in moves:
         move.start()
-    for copy in copies:
-        copy.start()
     for move in moves:
         move.wait()
 
@@ -130,10 +143,9 @@
         return panels[pl.ds(pl.multiple_of(place_ref[a, t], blk), blk)]
 
     for a in range(rows):
-        copies[a].wait()
         total = None
         for t in range(0, rounds, 2):
-            left = jnp.concatenate([blocks[a, t], blocks[a, t + 1]], axis=1)
+            left = jnp.concatenate([values_ref[t, a], values_ref[t + 1, a]], axis=1)
             right = jnp.concatenate([panel(a, t), panel(a, t + 1)], axis=0)
             term = jnp.dot(left, right, preferred_element_type=jnp.float32)
             total = term if total is None else total + term
@@ -149,17 +161,15 @@
         out_shape=jax.ShapeDtypeStruct((rows, blk + spare, width), jnp.bfloat16),
         in_specs=[
             pl.BlockSpec(memory_space=pltpu.SMEM),
-            any_space,
+            pl.BlockSpec(memory_space=pltpu.VMEM),
         ]
         + [any_space] * 5,
         out_specs=pl.BlockSpec(memory_space=pltpu.VMEM),
         scratch_shapes=[
             pltpu.VMEM((sum(PIECES) * blk, width), jnp.bfloat16),
-            pltpu.VMEM((rows, rounds, blk, blk), jnp.bfloat16),
             pltpu.SemaphoreType.DMA((5,)),
-            pltpu.SemaphoreType.DMA((rows,)),
         ],
-        compiler_params=pltpu.CompilerParams(vmem_limit_bytes=24 * 2**20),
+        compiler_params=pltpu.CompilerParams(vmem_limit_bytes=20 * 2**20),
         cost_estimate=pl.CostEstimate(
             flops=2 * rounds * rows * blk * blk * width, bytes_accessed=9 * 2**20, transcendentals=0
         ),
@@ -191,12 +201,14 @@
     inv_scale = 1.0 / math.sqrt(node_total)
     place = places(block_columns[0])
     panels, _ = gather_panels(features)
-    partial = panel_products(pltpu.with_memory_space_constraint(values, pltpu.HBM), place, panels)
+    blocks = loaded(values)
+    partial = panel_products(blocks, place, panels)
     hidden = summed_over_rep(partial).astype(jnp.bfloat16)
     hidden_grad, weight_part = dense_grads(hidden, weight, cotangent)
     n_rep = lax.axis_size(REP)
-    slices = lax.all_to_all(weight_part.reshape(n_rep, -1, f), REP, 0, 0, tiled=True)
-    weight_slice = jnp.sum(slices, axis=0).astype(jnp.bfloat16)
+    weight_part = weight_part.astype(jnp.bfloat16).reshape(n_rep, -1, f)
+    slices = lax.all_to_all(weight_part, REP, 0, 0, tiled=True)
+    weight_slice = jnp.sum(slices.astype(jnp.float32), axis=0).astype(jnp.bfloat16)
     panels, weight_slice = gather_panels(hidden_grad, weight_slice)
     extra = weight_slice.shape[0]
     back = panel_products(values, place, panels, extra)

time: 201 us -> 195 us (0.970)
  waiting for transfers between devices: 52.4 us -> 48 us
  Pallas kernels: 11.3 us -> 7.8 us
    pallas_call x2, Pallas kernels: 11.3 us -> 5.59 us  [panel_products(): pl.pallas_call(product_kernel, out_shape=jax.ShapeDtypeStruct((rows, blk...]
    ppermute x14, waiting for transfers between devices: 46.1 us -> 43 us  [shift(): return lax.ppermute(value, DOM + ('C',), pairs)]
    pallas_call x0 -> x1, Pallas kernels: none -> 2.2 us  [loaded(): pl.pallas_call(load_kernel, out_shape=jax.ShapeDtypeStruct(values.shape,...]
  transfers between devices with their start and end apart: 15 -> 15, of which waited for: 9 -> 10; matrix products, arithmetic and copies ran while one was open for 1% -> 1% of each run, Pallas kernels for 0% -> 1%
where the time goes in v1:
time: 195 us; the launch traced here: 194 us
  blocking collectives  73.1 us (37%)
  starting transfers between devices  59.4 us (30%)
  waiting for transfers between devices  48 us (25%)
  Pallas kernels  7.8 us (4%)
    ppermute x14, starting transfers between devices, shift(): return lax.ppermute(value, DOM + ('C',), pairs)  55.1 us
    ppermute x14, waiting for transfers between devices, shift(): return lax.ppermute(value, DOM + ('C',), pairs)  43 us
    all_gather x2, blocking collectives, gather_panels(): got = lax.all_gather(stacked([value], riding), 'ZH', axis=0, tiled=False)  42.4 us
    all_to_all x1, blocking collectives, shards(): received = lax.all_to_all(back, REP, 0, 0, tiled=True).astype(jnp.float32)  16 us
    all_to_all x1, blocking collectives, summed_over_rep(): received = lax.all_to_all(partial, REP, 0, 0, tiled=True)  14.6 us
    pallas_call x2, Pallas kernels, panel_products(): pl.pallas_call(product_kernel, out_shape=jax.ShapeDtypeStruct((rows, blk...  5.59 us
    all_to_all x1, waiting for transfers between devices, shards(): slices = lax.all_to_all(weight_part, REP, 0, 0, tiled=True)  5.07 us
    all_to_all x1, starting transfers between devices, shards(): slices = lax.all_to_all(weight_part, REP, 0, 0, tiled=True)  4.32 us
  transfers between devices with their start and end apart: 15, of which 10 were waited for; matrix products, arithmetic and copies ran while one was open for 1% of the time, Pallas kernels for 1%

profile of v1, /device:TPU:1, one launch (start us, length us, event | category | flops | bytes accessed | tf_op | source)
XLA Modules:
  0.0 194.3 jit_solution(7405025756202958511)
XLA Ops:
  0.6 0.0 copy-start
  0.6 25.6 %all-gather = bf16[512,256]{1,0:T(8,128)(2,1)S(1)} all-gather(bf16[128,256]{1,0:T(8,128)(2,1)} %param.7), channel_id=2, replica_groups=mesh['X'=4,'ZH'=4,'ZL'=4,'Y'=4,'C'=2] {'ZH'}, dimensions={0}, use_global_device_ids=true | all-gather | bytes 327680 | tf_op jit(solution)/shard_map/all_gather | solution.py:67
  26.2 4.6 %collective-permute-start = (bf16[512,256]{1,0:T(8,128)(2,1)S(1)}, bf16[512,256]{1,0:T(8,128)(2,1)S(1)}, u32[]{:S(2)}, u32[]{:S(2)}) collective-permute-start(bf16[512,256]{1,0:T(8,128)(2,1)S(1)} %all-gather), channel_id=1, source_target_pairs={{16,0},{257,1},{120,8},{265,9},{32,16},{273,17},{8,24},{281,25},{4... | collective-permute-start | bytes 786440 | tf_op jit(solution)/shard_map/ppermute | solution.py:47
  30.9 3.3 %collective-permute-start.1 = (bf16[512,256]{1,0:T(8,128)(2,1)S(1)}, bf16[512,256]{1,0:T(8,128)(2,1)S(1)}, u32[]{:S(2)}, u32[]{:S(2)}) collective-permute-start(bf16[512,256]{1,0:T(8,128)(2,1)S(1)} %all-gather), channel_id=1, source_target_pairs={{264,0},{145,1},{272,8},{153,9},{280,16},{161,17},{288,24},{169,25... | collective-permute-start | bytes 786440 | tf_op jit(solution)/shard_map/ppermute | solution.py:47
  34.2 3.8 %collective-permute-start.2 = (bf16[512,256]{1,0:T(8,128)(2,1)S(1)}, bf16[512,256]{1,0:T(8,128)(2,1)S(1)}, u32[]{:S(2)}, u32[]{:S(2)}) collective-permute-start(bf16[512,256]{1,0:T(8,128)(2,1)S(1)} %all-gather), channel_id=1, source_target_pairs={{376,0},{497,1},{256,8},{505,9},{264,16},{385,17},{272,24},{393,25... | collective-permute-start | bytes 786440 | tf_op jit(solution)/shard_map/ppermute | solution.py:47
  38.0 0.0 collective-permute-done
  38.0 6.7 %collective-permute-done.1 = bf16[512,256]{1,0:T(8,128)(2,1)S(1)} collective-permute-done((bf16[512,256]{1,0:T(8,128)(2,1)S(1)}, bf16[512,256]{1,0:T(8,128)(2,1)S(1)}, u32[]{:S(2)}, u32[]{:S(2)}) %collective-permute-start.1) | collective-permute-done | bytes 262176 | tf_op jit(solution)/shard_map/ppermute | solution.py:47
  44.8 2.8 %collective-permute-done.2 = bf16[512,256]{1,0:T(8,128)(2,1)S(1)} collective-permute-done((bf16[512,256]{1,0:T(8,128)(2,1)S(1)}, bf16[512,256]{1,0:T(8,128)(2,1)S(1)}, u32[]{:S(2)}, u32[]{:S(2)}) %collective-permute-start.2) | collective-permute-done | bytes 262176 | tf_op jit(solution)/shard_map/ppermute | solution.py:47
  47.6 7.8 %collective-permute-start.4 = (bf16[2048,256]{1,0:T(8,128)(2,1)S(1)}, bf16[2048,256]{1,0:T(8,128)(2,1)S(1)}, u32[]{:S(2)}, u32[]{:S(2)}) collective-permute-start(bf16[2048,256]{1,0:T(8,128)(2,1)S(1)} %constant_dynamic-update-slice_fusion.refs_0_), channel_id=1, source_target_pairs={{384,0},{121,1},{392,8},{1,9},{400,16},{9,17},{408,24},{17,25},{41... | collective-permute-start | bytes 3145736 | tf_op jit(solution)/shard_map/ppermute | solution.py:47
  55.4 1.9 collective-permute-start.3
  57.3 0.7 constant_dynamic-update-slice_fusion.5
  58.0 0.7 constant_dynamic-update-slice_fusion.4
  58.8 1.9 collective-permute-start.6
  60.7 4.6 %collective-permute-start.5 = (bf16[1024,256]{1,0:T(8,128)(2,1)}, bf16[1024,256]{1,0:T(8,128)(2,1)}, u32[]{:S(2)}, u32[]{:S(2)}) collective-permute-start(bf16[1024,256]{1,0:T(8,128)(2,1)} %constant_dynamic-update-slice_fusion.4), channel_id=1, source_target_pairs={{8,0},{129,1},{16,8},{137,9},{24,16},{145,17},{32,24},{153,25},{40... | collective-permute-start | bytes 1572872 | tf_op jit(solution)/shard_map/ppermute | solution.py:47
  65.3 0.0 copy-start.2
  65.3 2.2 %load_blocks.1.values_ref = bf16[16,8,128,128]{3,2,1,0:T(8,128)(2,1)S(1)} custom-call(bf16[16,8,128,128]{3,2,1,0:T(8,128)(2,1)} %bitcast.42), custom_call_target="tpu_custom_call" | custom-call | tf_op jit(solution)/shard_map/load_blocks/pallas_call | solution.py:114
  67.5 0.0 copy-done.2
  67.6 8.4 %collective-permute-done.6.refs_4_ = bf16[1024,256]{1,0:T(8,128)(2,1)} collective-permute-done((bf16[1024,256]{1,0:T(8,128)(2,1)}, bf16[1024,256]{1,0:T(8,128)(2,1)}, u32[]{:S(2)}, u32[]{:S(2)}) %collective-permute-start.6) | collective-permute-done | bytes 524320 | tf_op jit(solution)/shard_map/ppermute | solution.py:47
  76.0 1.3 collective-permute-done.5.refs_3_
  77.3 0.0 collective-permute-done.4.refs_2_
  77.3 0.0 collective-permute-done.3.refs_1_
  77.3 3.4 %panel_products.2 = bf16[8,128,256]{2,1,0:T(8,128)(2,1)S(1)} custom-call(s32[8,16]{1,0:T(8,128)S(1)} %fusion.20.place_ref, bf16[16,8,128,128]{3,2,1,0:T(8,128)(2,1)S(1)} %load_blocks.1.values_ref, bf16[2048,256]{1,0:T(8,128)(2,1)S(1)} %constant_dynamic-update-slice_fusion.refs_0_, bf16[2048,256]{1,0:T(8,128)(2,1)S(1)} %collective-permute-done.3.refs_1_, ...), custom_call_target="tpu_custom_call" | custom-call | flops 1073741824 | bytes 9437184 | tf_op jit(solution)/shard_map/panel_products/pallas_call | solution.py:159
  80.7 0.0 copy-start.3
  80.7 14.6 %all_to_all.15 = bf16[8,128,256]{2,1,0:T(8,128)(2,1)S(1)} all-to-all(bf16[8,128,256]{2,1,0:T(8,128)(2,1)S(1)} %panel_products.2), channel_id=1, replica_groups=mesh['X'=4,'ZH'=4,'ZL'=4,'Y'=4,'C'=2] {'Y','C'}, dimensions={0} | all-to-all | bytes 1048576 | tf_op jit(solution)/shard_map/all_to_all | solution.py:181
  95.3 0.1 reduce_sum.42
  95.4 0.0 copy-done
  95.4 0.0 copy-done.3
  95.4 0.2 multiply_convert_fusion
  95.6 0.9 convolution_convert_fusion
  96.5 4.3 %all-to-all-start.1 = ((bf16[8,32,256]{2,1,0:T(8,128)(2,1)}), bf16[8,32,256]{2,1,0:T(8,128)(2,1)S(1)}, u32[]{:S(2)}, u32[]{:S(2)}) async-start(bf16[8,32,256]{2,1,0:T(8,128)(2,1)} %bitcast.4), calls=%async_computation.1 | async-start | bytes 262144 | tf_op jit(solution)/shard_map/all_to_all | solution.py:210
  100.8 0.2 convolution_convert_fusion.1
  101.0 5.1 %all-to-all-done.1 = bf16[8,32,256]{2,1,0:T(8,128)(2,1)S(1)} async-done(((bf16[8,32,256]{2,1,0:T(8,128)(2,1)}), bf16[8,32,256]{2,1,0:T(8,128)(2,1)S(1)}, u32[]{:S(2)}, u32[]{:S(2)}) %all-to-all-start.1) | async-done | bytes 131104 | tf_op jit(solution)/shard_map/all_to_all | solution.py:210
  106.1 16.8 %all-gather.1 = bf16[640,256]{1,0:T(8,128)(2,1)S(1)} all-gather(bf16[160,256]{1,0:T(8,128)(2,1)S(1)} %pad_maximum_fusion.3), channel_id=3, replica_groups=mesh['X'=4,'ZH'=4,'ZL'=4,'Y'=4,'C'=2] {'ZH'}, dimensions={0}, use_global_device_ids=true | all-gather | bytes 409600 | tf_op jit(solution)/shard_map/all_gather | solution.py:67
  123.0 1.9 collective-permute-start.9
  125.0 7.6 %collective-permute-start.8 = (bf16[576,256]{1,0:T(8,128)(2,1)S(1)}, bf16[576,256]{1,0:T(8,128)(2,1)S(1)}, u32[]{:S(2)}, u32[]{:S(2)}) collective-permute-start(bf16[576,256]{1,0:T(8,128)(2,1)S(1)} %pad_maximum_fusion.2), channel_id=1, source_target_pairs={{264,0},{145,1},{272,8},{153,9},{280,16},{161,17},{288,24},{169,25... | collective-permute-start | bytes 884744 | tf_op jit(solution)/shard_map/ppermute | solution.py:47
  132.6 2.6 %collective-permute-start.7 = (bf16[576,256]{1,0:T(8,128)(2,1)S(1)}, bf16[576,256]{1,0:T(8,128)(2,1)S(1)}, u32[]{:S(2)}, u32[]{:S(2)}) collective-permute-start(bf16[576,256]{1,0:T(8,128)(2,1)S(1)} %pad_maximum_fusion.2), channel_id=1, source_target_pairs={{16,0},{257,1},{120,8},{265,9},{32,16},{273,17},{8,24},{281,25},{4... | collective-permute-start | bytes 884744 | tf_op jit(solution)/shard_map/ppermute | solution.py:47
  135.2 0.5 collective-permute-done.9
  135.8 1.3 collective-permute-done.8
  137.1 10.3 %collective-permute-done.7 = bf16[576,256]{1,0:T(8,128)(2,1)S(1)} collective-permute-done((bf16[576,256]{1,0:T(8,128)(2,1)S(1)}, bf16[576,256]{1,0:T(8,128)(2,1)S(1)}, u32[]{:S(2)}, u32[]{:S(2)}) %collective-permute-start.7) | collective-permute-done | bytes 294944 | tf_op jit(solution)/shard_map/ppermute | solution.py:47
  147.4 0.0 copy-start.1
  147.5 5.7 %collective-permute-start.11 = (bf16[2112,256]{1,0:T(8,128)(2,1)S(1)}, bf16[2112,256]{1,0:T(8,128)(2,1)S(1)}, u32[]{:S(2)}, u32[]{:S(2)}) collective-permute-start(bf16[2112,256]{1,0:T(8,128)(2,1)S(1)} %get-tuple-element.22.refs_0_), channel_id=1, source_target_pairs={{384,0},{121,1},{392,8},{1,9},{400,16},{9,17},{408,24},{17,25},{41... | collective-permute-start | bytes 3244040 | tf_op jit(solution)/shard_map/ppermute | solution.py:47
  153.2 1.9 collective-permute-start.10
  155.2 3.1 %collective-permute-start.13 = (bf16[1088,256]{1,0:T(8,128)(2,1)S(1)}, bf16[1088,256]{1,0:T(8,128)(2,1)S(1)}, u32[]{:S(2)}, u32[]{:S(2)}) collective-permute-start(bf16[1088,256]{1,0:T(8,128)(2,1)S(1)} %pad_maximum_fusion), channel_id=1, source_target_pairs={{120,0},{385,1},{0,8},{393,9},{8,16},{401,17},{16,24},{409,25},{24... | collective-permute-start | bytes 1671176 | tf_op jit(solution)/shard_map/ppermute | solution.py:47
  158.3 4.4 %collective-permute-start.12 = (bf16[1024,256]{1,0:T(8,128)(2,1)S(1)}, bf16[1024,256]{1,0:T(8,128)(2,1)S(1)}, u32[]{:S(2)}, u32[]{:S(2)}) collective-permute-start(bf16[1024,256]{1,0:T(8,128)(2,1)S(1)} %pad_maximum_fusion.1), channel_id=1, source_target_pairs={{8,0},{129,1},{16,8},{137,9},{24,16},{145,17},{32,24},{153,25},{40... | collective-permute-start | bytes 1572872 | tf_op jit(solution)/shard_map/ppermute | solution.py:47
  162.7 11.2 %collective-permute-done.13.refs_4_ = bf16[1088,256]{1,0:T(8,128)(2,1)S(1)} collective-permute-done((bf16[1088,256]{1,0:T(8,128)(2,1)S(1)}, bf16[1088,256]{1,0:T(8,128)(2,1)S(1)}, u32[]{:S(2)}, u32[]{:S(2)}) %collective-permute-start.13) | collective-permute-done | bytes 557088 | tf_op jit(solution)/shard_map/ppermute | solution.py:47
  173.9 0.0 collective-permute-done.11.refs_2_
  173.9 0.0 collective-permute-done.10.refs_1_
  174.0 0.4 collective-permute-done.12.refs_3_
  174.4 0.0 copy-done.1
  174.4 2.2 %panel_products.3 = bf16[8,160,256]{2,1,0:T(8,128)(2,1)S(1)} custom-call(s32[8,16]{1,0:T(8,128)S(1)} %fusion.20.place_ref, bf16[16,8,128,128]{3,2,1,0:T(8,128)(2,1)S(1)} %bitcast.43, bf16[2112,256]{1,0:T(8,128)(2,1)S(1)} %get-tuple-element.22.refs_0_, bf16[2112,256]{1,0:T(8,128)(2,1)S(1)} %collective-permute-done.10.refs_1_, ...), custom_call_target="tpu_custom_call" | custom-call | flops 1073741824 | bytes 9437184 | tf_op jit(solution)/shard_map/panel_products/pallas_call | solution.py:159
  176.7 16.0 %all_to_all.16 = bf16[8,160,256]{2,1,0:T(8,128)(2,1)S(1)} all-to-all(bf16[8,160,256]{2,1,0:T(8,128)(2,1)S(1)} %broadcast_dynamic-update-slice_fusion), channel_id=1, replica_groups=mesh['X'=4,'ZH'=4,'ZL'=4,'Y'=4,'C'=2] {'Y','C'}, dimensions={0} | all-to-all | bytes 1310720 | tf_op jit(solution)/shard_map/all_to_all | solution.py:216
  192.7 0.1 convert_element_type.68
  192.8 0.7 slice_reduce_fusion
  193.5 0.7 slice_multiply_fusion
  (29 shorter events, 0.5 us)
Async XLA Ops:
  0.6 94.8 %copy-start = (bf16[256,256]{1,0:T(8,128)(2,1)S(1)}, bf16[256,256]{1,0:T(8,128)(2,1)}, u32[]{:S(2)}) copy-start(bf16[256,256]{1,0:T(8,128)(2,1)} %param.10) | copy-start | bytes 393220
  26.2 11.8 %collective-permute-start = (bf16[512,256]{1,0:T(8,128)(2,1)S(1)}, bf16[512,256]{1,0:T(8,128)(2,1)S(1)}, u32[]{:S(2)}, u32[]{:S(2)}) collective-permute-start(bf16[512,256]{1,0:T(8,128)(2,1)S(1)} %all-gather), channel_id=1, source_target_pairs={{16,0},{257,1},{120,8},{265,9},{32,16},{273,17},{8,24},{281,25},{4... | collective-permute-start | bytes 786440 | tf_op jit(solution)/shard_map/ppermute | solution.py:47
  30.9 13.9 %collective-permute-start.1 = (bf16[512,256]{1,0:T(8,128)(2,1)S(1)}, bf16[512,256]{1,0:T(8,128)(2,1)S(1)}, u32[]{:S(2)}, u32[]{:S(2)}) collective-permute-start(bf16[512,256]{1,0:T(8,128)(2,1)S(1)} %all-gather), channel_id=1, source_target_pairs={{264,0},{145,1},{272,8},{153,9},{280,16},{161,17},{288,24},{169,25... | collective-permute-start | bytes 786440 | tf_op jit(solution)/shard_map/ppermute | solution.py:47
  34.2 13.4 %collective-permute-start.2 = (bf16[512,256]{1,0:T(8,128)(2,1)S(1)}, bf16[512,256]{1,0:T(8,128)(2,1)S(1)}, u32[]{:S(2)}, u32[]{:S(2)}) collective-permute-start(bf16[512,256]{1,0:T(8,128)(2,1)S(1)} %all-gather), channel_id=1, source_target_pairs={{376,0},{497,1},{256,8},{505,9},{264,16},{385,17},{272,24},{393,25... | collective-permute-start | bytes 786440 | tf_op jit(solution)/shard_map/ppermute | solution.py:47
  47.6 29.7 %collective-permute-start.4 = (bf16[2048,256]{1,0:T(8,128)(2,1)S(1)}, bf16[2048,256]{1,0:T(8,128)(2,1)S(1)}, u32[]{:S(2)}, u32[]{:S(2)}) collective-permute-start(bf16[2048,256]{1,0:T(8,128)(2,1)S(1)} %constant_dynamic-update-slice_fusion.refs_0_), channel_id=1, source_target_pairs={{384,0},{121,1},{392,8},{1,9},{400,16},{9,17},{408,24},{17,25},{41... | collective-permute-start | bytes 3145736 | tf_op jit(solution)/shard_map/ppermute | solution.py:47
  55.4 21.9 %collective-permute-start.3 = (bf16[2048,256]{1,0:T(8,128)(2,1)S(1)}, bf16[2048,256]{1,0:T(8,128)(2,1)S(1)}, u32[]{:S(2)}, u32[]{:S(2)}) collective-permute-start(bf16[2048,256]{1,0:T(8,128)(2,1)S(1)} %constant_dynamic-update-slice_fusion.refs_0_), channel_id=1, source_target_pairs={{128,0},{9,1},{136,8},{17,9},{144,16},{25,17},{152,24},{33,25},{16... | collective-permute-start | bytes 3145736 | tf_op jit(solution)/shard_map/ppermute | solution.py:47
  58.8 17.2 %collective-permute-start.6 = (bf16[1024,256]{1,0:T(8,128)(2,1)}, bf16[1024,256]{1,0:T(8,128)(2,1)}, u32[]{:S(2)}, u32[]{:S(2)}) collective-permute-start(bf16[1024,256]{1,0:T(8,128)(2,1)} %constant_dynamic-update-slice_fusion.4), channel_id=1, source_target_pairs={{120,0},{385,1},{0,8},{393,9},{8,16},{401,17},{16,24},{409,25},{24... | collective-permute-start | bytes 1572872 | tf_op jit(solution)/shard_map/ppermute | solution.py:47
  60.7 16.6 %collective-permute-start.5 = (bf16[1024,256]{1,0:T(8,128)(2,1)}, bf16[1024,256]{1,0:T(8,128)(2,1)}, u32[]{:S(2)}, u32[]{:S(2)}) collective-permute-start(bf16[1024,256]{1,0:T(8,128)(2,1)} %constant_dynamic-update-slice_fusion.4), channel_id=1, source_target_pairs={{8,0},{129,1},{16,8},{137,9},{24,16},{145,17},{32,24},{153,25},{40... | collective-permute-start | bytes 1572872 | tf_op jit(solution)/shard_map/ppermute | solution.py:47
  65.3 2.2 %copy-start.2 = (s32[1,16,8]{1,2,0:T(8,128)S(1)}, s32[1,16,8]{1,2,0:T(8,128)}, u32[]{:S(2)}) copy-start(s32[1,16,8]{1,2,0:T(8,128)} %param.9) | copy-start | bytes 1540
  80.7 14.7 %copy-start.3 = (bf16[128,256]{1,0:T(8,128)(2,1)S(1)}, bf16[128,256]{1,0:T(8,128)(2,1)}, u32[]{:S(2)}) copy-start(bf16[128,256]{1,0:T(8,128)(2,1)} %param.11) | copy-start | bytes 196612
  96.5 9.6 %all-to-all-start.1 = ((bf16[8,32,256]{2,1,0:T(8,128)(2,1)}), bf16[8,32,256]{2,1,0:T(8,128)(2,1)S(1)}, u32[]{:S(2)}, u32[]{:S(2)}) async-start(bf16[8,32,256]{2,1,0:T(8,128)(2,1)} %bitcast.4), calls=%async_computation.1 | async-start | bytes 262144 | tf_op jit(solution)/shard_map/all_to_all | solution.py:210
  123.0 12.7 %collective-permute-start.9 = (bf16[576,256]{1,0:T(8,128)(2,1)S(1)}, bf16[576,256]{1,0:T(8,128)(2,1)S(1)}, u32[]{:S(2)}, u32[]{:S(2)}) collective-permute-start(bf16[576,256]{1,0:T(8,128)(2,1)S(1)} %pad_maximum_fusion.2), channel_id=1, source_target_pairs={{376,0},{497,1},{256,8},{505,9},{264,16},{385,17},{272,24},{393,25... | collective-permute-start | bytes 884744 | tf_op jit(solution)/shard_map/ppermute | solution.py:47
  125.0 12.1 %collective-permute-start.8 = (bf16[576,256]{1,0:T(8,128)(2,1)S(1)}, bf16[576,256]{1,0:T(8,128)(2,1)S(1)}, u32[]{:S(2)}, u32[]{:S(2)}) collective-permute-start(bf16[576,256]{1,0:T(8,128)(2,1)S(1)} %pad_maximum_fusion.2), channel_id=1, source_target_pairs={{264,0},{145,1},{272,8},{153,9},{280,16},{161,17},{288,24},{169,25... | collective-permute-start | bytes 884744 | tf_op jit(solution)/shard_map/ppermute | solution.py:47
  132.6 14.8 %collective-permute-start.7 = (bf16[576,256]{1,0:T(8,128)(2,1)S(1)}, bf16[576,256]{1,0:T(8,128)(2,1)S(1)}, u32[]{:S(2)}, u32[]{:S(2)}) collective-permute-start(bf16[576,256]{1,0:T(8,128)(2,1)S(1)} %pad_maximum_fusion.2), channel_id=1, source_target_pairs={{16,0},{257,1},{120,8},{265,9},{32,16},{273,17},{8,24},{281,25},{4... | collective-permute-start | bytes 884744 | tf_op jit(solution)/shard_map/ppermute | solution.py:47
  147.4 27.0 %copy-start.1 = (bf16[1,16,8,128,128]{4,3,2,1,0:T(8,128)(2,1)S(1)}, bf16[1,16,8,128,128]{4,3,2,1,0:T(8,128)(2,1)}, u32[]{:S(2)}) copy-start(bf16[1,16,8,128,128]{4,3,2,1,0:T(8,128)(2,1)} %param.8) | copy-start | bytes 12582916
  147.5 26.4 %collective-permute-start.11 = (bf16[2112,256]{1,0:T(8,128)(2,1)S(1)}, bf16[2112,256]{1,0:T(8,128)(2,1)S(1)}, u32[]{:S(2)}, u32[]{:S(2)}) collective-permute-start(bf16[2112,256]{1,0:T(8,128)(2,1)S(1)} %get-tuple-element.22.refs_0_), channel_id=1, source_target_pairs={{384,0},{121,1},{392,8},{1,9},{400,16},{9,17},{408,24},{17,25},{41... | collective-permute-start | bytes 3244040 | tf_op jit(solution)/shard_map/ppermute | solution.py:47
  153.2 20.7 %collective-permute-start.10 = (bf16[2112,256]{1,0:T(8,128)(2,1)S(1)}, bf16[2112,256]{1,0:T(8,128)(2,1)S(1)}, u32[]{:S(2)}, u32[]{:S(2)}) collective-permute-start(bf16[2112,256]{1,0:T(8,128)(2,1)S(1)} %get-tuple-element.22.refs_0_), channel_id=1, source_target_pairs={{128,0},{9,1},{136,8},{17,9},{144,16},{25,17},{152,24},{33,25},{16... | collective-permute-start | bytes 3244040 | tf_op jit(solution)/shard_map/ppermute | solution.py:47
  155.2 18.7 %collective-permute-start.13 = (bf16[1088,256]{1,0:T(8,128)(2,1)S(1)}, bf16[1088,256]{1,0:T(8,128)(2,1)S(1)}, u32[]{:S(2)}, u32[]{:S(2)}) collective-permute-start(bf16[1088,256]{1,0:T(8,128)(2,1)S(1)} %pad_maximum_fusion), channel_id=1, source_target_pairs={{120,0},{385,1},{0,8},{393,9},{8,16},{401,17},{16,24},{409,25},{24... | collective-permute-start | bytes 1671176 | tf_op jit(solution)/shard_map/ppermute | solution.py:47
  158.3 16.1 %collective-permute-start.12 = (bf16[1024,256]{1,0:T(8,128)(2,1)S(1)}, bf16[1024,256]{1,0:T(8,128)(2,1)S(1)}, u32[]{:S(2)}, u32[]{:S(2)}) collective-permute-start(bf16[1024,256]{1,0:T(8,128)(2,1)S(1)} %pad_maximum_fusion.1), channel_id=1, source_target_pairs={{8,0},{129,1},{16,8},{137,9},{24,16},{145,17},{32,24},{153,25},{40... | collective-permute-start | bytes 1572872 | tf_op jit(solution)/shard_map/ppermute | solution.py:47

commit v2 on v1

--- a/solution.py
+++ b/solution.py
@@ -1,3 +1,4 @@
+import functools
 import math
 
 import jax
@@ -14,7 +15,7 @@
 REP = ("Y", "C")
 N_X, N_Z, FOUR = 4, 16, 4
 
-SECOND = (((0, 2), (2, 1), (2, -1)), ((2, 0), (1, 2), (-1, -2)))
+SECOND = (((2, 1), (0, 2), (2, -1)), ((1, 2), (2, 0), (-1, -2)))
 THIRD = (((1, 0), (-1, 0), (0, 1), (0, -1)), ((0, 1), (0, -1), (1, 0), (-1, 0)))
 PIECES = (16, 16, 16, 8, 8)
 BLK = 128
@@ -25,7 +26,7 @@
     table = {k: 4 * i for i, k in enumerate(held)}
     at = PIECES[0]
     for i, (dx, dz) in enumerate(THIRD[core]):
-        sent = held if i < 2 else (held[0], held[2])
+        sent = held if i < 2 else held[:2]
         for hx, hz in sent:
             table[(hx + dx, hz + dz)] = at
             at += 4
@@ -77,17 +78,17 @@
         terms = [whole(pair)]
         for m in more:
             terms.append(whole(m[size:]))
-        pair = halves((terms[0] + terms[1]) + (terms[2] + terms[3]))
+        pair = halves((terms[0] + terms[2]) + (terms[1] + terms[3]))
     held = stacked([own] + [m[:size] for m in more], pair)
-    half = jnp.concatenate(lax.optimization_barrier([own, more[1][:size]]), axis=0)
+    half = jnp.concatenate(lax.optimization_barrier([own, more[0][:size]]), axis=0)
     near = []
     for i, steps in enumerate(zip(*THIRD)):
-        sent = held if i < 2 else half if i == 2 else stacked([half], pair)
-        near.append(shift(sent, *steps))
+        near.append(shift(held if i < 2 else half, *steps))
     total = None
     if riding is not None:
+        side = whole(shift(pair, *list(zip(*THIRD))[2]))
         n = pair.shape[0]
-        plus, minus, side = (whole(near[i][-n:]) for i in (0, 1, 3))
+        plus, minus = (whole(v[-n:]) for v in near[:2])
         total = (whole(pair) + side) + (plus + minus)
     return (held, *near), total
 
@@ -182,6 +183,31 @@
     return jnp.sum(received.astype(jnp.float32), axis=0)
 
 
+def tail_kernel(scale, received_ref, sum_ref, slice_ref):
+    rows = sum_ref.shape[0]
+    total = received_ref[0, 0:rows].astype(jnp.float32)
+    for i in range(1, received_ref.shape[0]):
+        total = total + received_ref[i, 0:rows].astype(jnp.float32)
+    sum_ref[...] = total.astype(sum_ref.dtype)
+    for i in range(received_ref.shape[0]):
+        slice_ref[i] = received_ref[i, rows:].astype(jnp.float32) * scale
+
+
+def tail(received, rows, scale):
+    n, high, width = received.shape
+    return pl.pallas_call(
+        functools.partial(tail_kernel, scale),
+        out_shape=(
+            jax.ShapeDtypeStruct((rows, width), jnp.bfloat16),
+            jax.ShapeDtypeStruct((n, high - rows, width), jnp.float32),
+        ),
+        in_specs=[pl.BlockSpec(memory_space=pltpu.VMEM)],
+        out_specs=(pl.BlockSpec(memory_space=pltpu.VMEM),) * 2,
+        compiler_params=pltpu.CompilerParams(vmem_limit_bytes=8 * 2**20),
+        name="tail",
+    )(received)
+
+
 def dense_grads(hidden, weight, cotangent):
     pre_act = jnp.dot(hidden, weight, preferred_element_type=jnp.float32)
     sigmoid_value = jax.nn.sigmoid(pre_act)
@@ -213,10 +239,9 @@
     extra = weight_slice.shape[0]
     back = panel_products(values, place, panels, extra)
     back = back.at[:, rows:].set(weight_slice.astype(jnp.bfloat16)[None])
-    received = lax.all_to_all(back, REP, 0, 0, tiled=True).astype(jnp.float32)
-    feature_grad = jnp.sum(received[:, :rows], axis=0).astype(jnp.bfloat16)
-    weight_grad = received[:, rows:].reshape(f, f) * inv_scale
-    return feature_grad, weight_grad
+    received = lax.all_to_all(back, REP, 0, 0, tiled=True)
+    feature_grad, weight_grad = tail(received, rows, inv_scale)
+    return feature_grad, weight_grad.reshape(f, f)
 
 
 def solution(mesh):

time: 195 us -> 196 us (level)
  waiting for transfers between devices: 48 us -> 46 us
    all_gather x2, blocking collectives: 42.4 us -> 45.5 us  [gather_panels(): got = lax.all_gather(stacked([value], riding), 'ZH', axis=0, tiled=False)]
    all_to_all x1, blocking collectives: 16 us -> 13.2 us  [shards(): received = lax.all_to_all(back, REP, 0, 0, tiled=True)]
    ppermute x14 -> x15, waiting for transfers between devices: 43 us -> 40.9 us  [shift(): return lax.ppermute(value, DOM + ('C',), pairs)]
    ppermute x14 -> x15, starting transfers between devices: 55.1 us -> 56.9 us  [shift(): return lax.ppermute(value, DOM + ('C',), pairs)]
  transfers between devices with their start and end apart: 15 -> 16, of which waited for: 10 -> 13; matrix products, arithmetic and copies ran while one was open for 1% -> 1% of each run, Pallas kernels for 1% -> 1%
where the time goes in v2:
time: 196 us; the launch traced here: 195 us
  blocking collectives  74.5 us (38%)
  starting transfers between devices  61.2 us (31%)
  waiting for transfers between devices  46 us (23%)
  Pallas kernels  8.59 us (4%)
    ppermute x15, starting transfers between devices, shift(): return lax.ppermute(value, DOM + ('C',), pairs)  56.9 us
    all_gather x2, blocking collectives, gather_panels(): got = lax.all_gather(stacked([value], riding), 'ZH', axis=0, tiled=False)  45.5 us
    ppermute x15, waiting for transfers between devices, shift(): return lax.ppermute(value, DOM + ('C',), pairs)  40.9 us
    all_to_all x1, blocking collectives, summed_over_rep(): received = lax.all_to_all(partial, REP, 0, 0, tiled=True)  15.7 us
    all_to_all x1, blocking collectives, shards(): received = lax.all_to_all(back, REP, 0, 0, tiled=True)  13.2 us
    pallas_call x2, Pallas kernels, panel_products(): pl.pallas_call(product_kernel, out_shape=jax.ShapeDtypeStruct((rows, blk...  5.6 us
    all_to_all x1, waiting for transfers between devices, shards(): slices = lax.all_to_all(weight_part, REP, 0, 0, tiled=True)  5.07 us
    all_to_all x1, starting transfers between devices, shards(): slices = lax.all_to_all(weight_part, REP, 0, 0, tiled=True)  4.32 us
  transfers between devices with their start and end apart: 16, of which 13 were waited for; matrix products, arithmetic and copies ran while one was open for 1% of the time, Pallas kernels for 1%

profile of v2, /device:TPU:1, one launch (start us, length us, event | category | flops | bytes accessed | tf_op | source)
XLA Modules:
  0.0 194.6 jit_solution(3597124787282413995)
XLA Ops:
  0.6 0.0 copy-start
  0.6 25.6 %all-gather = bf16[512,256]{1,0:T(8,128)(2,1)S(1)} all-gather(bf16[128,256]{1,0:T(8,128)(2,1)} %param.7), channel_id=2, replica_groups=mesh['X'=4,'ZH'=4,'ZL'=4,'Y'=4,'C'=2] {'ZH'}, dimensions={0}, use_global_device_ids=true | all-gather | bytes 327680 | tf_op jit(solution)/shard_map/all_gather | solution.py:68
  26.2 4.9 %collective-permute-start = (bf16[512,256]{1,0:T(8,128)(2,1)S(1)}, bf16[512,256]{1,0:T(8,128)(2,1)S(1)}, u32[]{:S(2)}, u32[]{:S(2)}) collective-permute-start(bf16[512,256]{1,0:T(8,128)(2,1)S(1)} %all-gather), channel_id=1, source_target_pairs={{264,0},{145,1},{272,8},{153,9},{280,16},{161,17},{288,24},{169,25... | collective-permute-start | bytes 786440 | tf_op jit(solution)/shard_map/ppermute | solution.py:48
  31.2 2.4 %collective-permute-start.1 = (bf16[512,256]{1,0:T(8,128)(2,1)S(1)}, bf16[512,256]{1,0:T(8,128)(2,1)S(1)}, u32[]{:S(2)}, u32[]{:S(2)}) collective-permute-start(bf16[512,256]{1,0:T(8,128)(2,1)S(1)} %all-gather), channel_id=1, source_target_pairs={{16,0},{257,1},{120,8},{265,9},{32,16},{273,17},{8,24},{281,25},{4... | collective-permute-start | bytes 786440 | tf_op jit(solution)/shard_map/ppermute | solution.py:48
  33.6 3.8 %collective-permute-start.2 = (bf16[512,256]{1,0:T(8,128)(2,1)S(1)}, bf16[512,256]{1,0:T(8,128)(2,1)S(1)}, u32[]{:S(2)}, u32[]{:S(2)}) collective-permute-start(bf16[512,256]{1,0:T(8,128)(2,1)S(1)} %all-gather), channel_id=1, source_target_pairs={{376,0},{497,1},{256,8},{505,9},{264,16},{385,17},{272,24},{393,25... | collective-permute-start | bytes 786440 | tf_op jit(solution)/shard_map/ppermute | solution.py:48
  37.4 1.7 collective-permute-done
  39.1 5.3 %collective-permute-done.1 = bf16[512,256]{1,0:T(8,128)(2,1)S(1)} collective-permute-done((bf16[512,256]{1,0:T(8,128)(2,1)S(1)}, bf16[512,256]{1,0:T(8,128)(2,1)S(1)}, u32[]{:S(2)}, u32[]{:S(2)}) %collective-permute-start.1) | collective-permute-done | bytes 262176 | tf_op jit(solution)/shard_map/ppermute | solution.py:48
  44.5 5.8 %collective-permute-done.2 = bf16[512,256]{1,0:T(8,128)(2,1)S(1)} collective-permute-done((bf16[512,256]{1,0:T(8,128)(2,1)S(1)}, bf16[512,256]{1,0:T(8,128)(2,1)S(1)}, u32[]{:S(2)}, u32[]{:S(2)}) %collective-permute-start.2) | collective-permute-done | bytes 262176 | tf_op jit(solution)/shard_map/ppermute | solution.py:48
  50.3 4.2 %collective-permute-start.4 = (bf16[2048,256]{1,0:T(8,128)(2,1)S(1)}, bf16[2048,256]{1,0:T(8,128)(2,1)S(1)}, u32[]{:S(2)}, u32[]{:S(2)}) collective-permute-start(bf16[2048,256]{1,0:T(8,128)(2,1)S(1)} %constant_dynamic-update-slice_fusion.refs_0_), channel_id=1, source_target_pairs={{384,0},{121,1},{392,8},{1,9},{400,16},{9,17},{408,24},{17,25},{41... | collective-permute-start | bytes 3145736 | tf_op jit(solution)/shard_map/ppermute | solution.py:48
  54.5 2.3 %collective-permute-start.3 = (bf16[2048,256]{1,0:T(8,128)(2,1)S(1)}, bf16[2048,256]{1,0:T(8,128)(2,1)S(1)}, u32[]{:S(2)}, u32[]{:S(2)}) collective-permute-start(bf16[2048,256]{1,0:T(8,128)(2,1)S(1)} %constant_dynamic-update-slice_fusion.refs_0_), channel_id=1, source_target_pairs={{128,0},{9,1},{136,8},{17,9},{144,16},{25,17},{152,24},{33,25},{16... | collective-permute-start | bytes 3145736 | tf_op jit(solution)/shard_map/ppermute | solution.py:48
  56.8 0.7 constant_dynamic-update-slice_fusion.5
  57.5 0.7 constant_dynamic-update-slice_fusion.4
  58.3 1.9 collective-permute-start.6
  60.2 4.6 %collective-permute-start.5 = (bf16[1024,256]{1,0:T(8,128)(2,1)}, bf16[1024,256]{1,0:T(8,128)(2,1)}, u32[]{:S(2)}, u32[]{:S(2)}) collective-permute-start(bf16[1024,256]{1,0:T(8,128)(2,1)} %constant_dynamic-update-slice_fusion.4), channel_id=1, source_target_pairs={{8,0},{129,1},{16,8},{137,9},{24,16},{145,17},{32,24},{153,25},{40... | collective-permute-start | bytes 1572872 | tf_op jit(solution)/shard_map/ppermute | solution.py:48
  64.8 0.0 copy-start.2
  64.8 2.2 %load_blocks.1.values_ref = bf16[16,8,128,128]{3,2,1,0:T(8,128)(2,1)S(1)} custom-call(bf16[16,8,128,128]{3,2,1,0:T(8,128)(2,1)} %bitcast.42), custom_call_target="tpu_custom_call" | custom-call | tf_op jit(solution)/shard_map/load_blocks/pallas_call | solution.py:115
  67.0 0.0 copy-done.2
  67.1 8.4 %collective-permute-done.6.refs_4_ = bf16[1024,256]{1,0:T(8,128)(2,1)} collective-permute-done((bf16[1024,256]{1,0:T(8,128)(2,1)}, bf16[1024,256]{1,0:T(8,128)(2,1)}, u32[]{:S(2)}, u32[]{:S(2)}) %collective-permute-start.6) | collective-permute-done | bytes 524320 | tf_op jit(solution)/shard_map/ppermute | solution.py:48
  75.5 1.3 collective-permute-done.5.refs_3_
  76.8 0.0 collective-permute-done.4.refs_2_
  76.8 0.0 collective-permute-done.3.refs_1_
  76.8 3.4 %panel_products.2 = bf16[8,128,256]{2,1,0:T(8,128)(2,1)S(1)} custom-call(s32[8,16]{1,0:T(8,128)S(1)} %fusion.20.place_ref, bf16[16,8,128,128]{3,2,1,0:T(8,128)(2,1)S(1)} %load_blocks.1.values_ref, bf16[2048,256]{1,0:T(8,128)(2,1)S(1)} %constant_dynamic-update-slice_fusion.refs_0_, bf16[2048,256]{1,0:T(8,128)(2,1)S(1)} %collective-permute-done.3.refs_1_, ...), custom_call_target="tpu_custom_call" | custom-call | flops 1073741824 | bytes 9437184 | tf_op jit(solution)/shard_map/panel_products/pallas_call | solution.py:160
  80.2 0.0 copy-start.3
  80.2 15.7 %all_to_all.15 = bf16[8,128,256]{2,1,0:T(8,128)(2,1)S(1)} all-to-all(bf16[8,128,256]{2,1,0:T(8,128)(2,1)S(1)} %panel_products.2), channel_id=1, replica_groups=mesh['X'=4,'ZH'=4,'ZL'=4,'Y'=4,'C'=2] {'Y','C'}, dimensions={0} | all-to-all | bytes 1048576 | tf_op jit(solution)/shard_map/all_to_all | solution.py:182
  95.9 0.1 reduce_sum.33
  96.0 0.0 copy-done
  96.0 0.0 copy-done.3
  96.0 0.2 multiply_convert_fusion
  96.2 0.9 convolution_convert_fusion
  97.1 4.3 %all-to-all-start.1 = ((bf16[8,32,256]{2,1,0:T(8,128)(2,1)}), bf16[8,32,256]{2,1,0:T(8,128)(2,1)S(1)}, u32[]{:S(2)}, u32[]{:S(2)}) async-start(bf16[8,32,256]{2,1,0:T(8,128)(2,1)} %bitcast.4), calls=%async_computation.1 | async-start | bytes 262144 | tf_op jit(solution)/shard_map/all_to_all | solution.py:236
  101.4 0.2 convolution_convert_fusion.1
  101.6 5.1 %all-to-all-done.1 = bf16[8,32,256]{2,1,0:T(8,128)(2,1)S(1)} async-done(((bf16[8,32,256]{2,1,0:T(8,128)(2,1)}), bf16[8,32,256]{2,1,0:T(8,128)(2,1)S(1)}, u32[]{:S(2)}, u32[]{:S(2)}) %all-to-all-start.1) | async-done | bytes 131104 | tf_op jit(solution)/shard_map/all_to_all | solution.py:236
  106.7 19.9 %all-gather.1 = bf16[640,256]{1,0:T(8,128)(2,1)S(1)} all-gather(bf16[160,256]{1,0:T(8,128)(2,1)S(1)} %pad_maximum_fusion.1), channel_id=3, replica_groups=mesh['X'=4,'ZH'=4,'ZL'=4,'Y'=4,'C'=2] {'ZH'}, dimensions={0}, use_global_device_ids=true | all-gather | bytes 409600 | tf_op jit(solution)/shard_map/all_gather | solution.py:68
  126.7 1.9 collective-permute-start.9
  128.6 4.4 %collective-permute-start.8 = (bf16[576,256]{1,0:T(8,128)(2,1)S(1)}, bf16[576,256]{1,0:T(8,128)(2,1)S(1)}, u32[]{:S(2)}, u32[]{:S(2)}) collective-permute-start(bf16[576,256]{1,0:T(8,128)(2,1)S(1)} %pad_maximum_fusion), channel_id=1, source_target_pairs={{16,0},{257,1},{120,8},{265,9},{32,16},{273,17},{8,24},{281,25},{4... | collective-permute-start | bytes 884744 | tf_op jit(solution)/shard_map/ppermute | solution.py:48
  133.0 7.0 %collective-permute-start.7 = (bf16[576,256]{1,0:T(8,128)(2,1)S(1)}, bf16[576,256]{1,0:T(8,128)(2,1)S(1)}, u32[]{:S(2)}, u32[]{:S(2)}) collective-permute-start(bf16[576,256]{1,0:T(8,128)(2,1)S(1)} %pad_maximum_fusion), channel_id=1, source_target_pairs={{264,0},{145,1},{272,8},{153,9},{280,16},{161,17},{288,24},{169,25... | collective-permute-start | bytes 884744 | tf_op jit(solution)/shard_map/ppermute | solution.py:48
  140.0 4.0 %collective-permute-done.9 = bf16[576,256]{1,0:T(8,128)(2,1)S(1)} collective-permute-done((bf16[576,256]{1,0:T(8,128)(2,1)S(1)}, bf16[576,256]{1,0:T(8,128)(2,1)S(1)}, u32[]{:S(2)}, u32[]{:S(2)}) %collective-permute-start.9) | collective-permute-done | bytes 294944 | tf_op jit(solution)/shard_map/ppermute | solution.py:48
  144.1 0.1 collective-permute-done.8
  144.2 0.0 copy-start.1
  144.2 4.2 %collective-permute-done.7 = bf16[576,256]{1,0:T(8,128)(2,1)S(1)} collective-permute-done((bf16[576,256]{1,0:T(8,128)(2,1)S(1)}, bf16[576,256]{1,0:T(8,128)(2,1)S(1)}, u32[]{:S(2)}, u32[]{:S(2)}) %collective-permute-start.7) | collective-permute-done | bytes 294944 | tf_op jit(solution)/shard_map/ppermute | solution.py:48
  148.6 4.0 %collective-permute-start.11 = (bf16[2112,256]{1,0:T(8,128)(2,1)S(1)}, bf16[2112,256]{1,0:T(8,128)(2,1)S(1)}, u32[]{:S(2)}, u32[]{:S(2)}) collective-permute-start(bf16[2112,256]{1,0:T(8,128)(2,1)S(1)} %get-tuple-element.26.refs_0_), channel_id=1, source_target_pairs={{384,0},{121,1},{392,8},{1,9},{400,16},{9,17},{408,24},{17,25},{41... | collective-permute-start | bytes 3244040 | tf_op jit(solution)/shard_map/ppermute | solution.py:48
  152.5 5.9 %collective-permute-start.10 = (bf16[2112,256]{1,0:T(8,128)(2,1)S(1)}, bf16[2112,256]{1,0:T(8,128)(2,1)S(1)}, u32[]{:S(2)}, u32[]{:S(2)}) collective-permute-start(bf16[2112,256]{1,0:T(8,128)(2,1)S(1)} %get-tuple-element.26.refs_0_), channel_id=1, source_target_pairs={{128,0},{9,1},{136,8},{17,9},{144,16},{25,17},{152,24},{33,25},{16... | collective-permute-start | bytes 3244040 | tf_op jit(solution)/shard_map/ppermute | solution.py:48
  158.5 3.2 %collective-permute-start.14 = (bf16[64,256]{1,0:T(8,128)(2,1)S(1)}, bf16[64,256]{1,0:T(8,128)(2,1)S(1)}, u32[]{:S(2)}, u32[]{:S(2)}) collective-permute-start(bf16[64,256]{1,0:T(8,128)(2,1)S(1)} %get-tuple-element.34), channel_id=1, source_target_pairs={{8,0},{129,1},{16,8},{137,9},{24,16},{145,17},{32,24},{153,25},{40... | collective-permute-start | bytes 98312 | tf_op jit(solution)/shard_map/ppermute | solution.py:48
  161.7 2.1 %collective-permute-start.13 = (bf16[1024,256]{1,0:T(8,128)(2,1)S(1)}, bf16[1024,256]{1,0:T(8,128)(2,1)S(1)}, u32[]{:S(2)}, u32[]{:S(2)}) collective-permute-start(bf16[1024,256]{1,0:T(8,128)(2,1)S(1)} %constant_dynamic-update-slice_fusion.10), channel_id=1, source_target_pairs={{120,0},{385,1},{0,8},{393,9},{8,16},{401,17},{16,24},{409,25},{24... | collective-permute-start | bytes 1572872 | tf_op jit(solution)/shard_map/ppermute | solution.py:48
  163.8 4.4 %collective-permute-start.12 = (bf16[1024,256]{1,0:T(8,128)(2,1)S(1)}, bf16[1024,256]{1,0:T(8,128)(2,1)S(1)}, u32[]{:S(2)}, u32[]{:S(2)}) collective-permute-start(bf16[1024,256]{1,0:T(8,128)(2,1)S(1)} %constant_dynamic-update-slice_fusion.10), channel_id=1, source_target_pairs={{8,0},{129,1},{16,8},{137,9},{24,16},{145,17},{32,24},{153,25},{40... | collective-permute-start | bytes 1572872 | tf_op jit(solution)/shard_map/ppermute | solution.py:48
  168.2 0.0 collective-permute-done.14
  168.2 1.3 collective-permute-done.11.refs_2_
  169.5 1.6 collective-permute-done.10.refs_1_
  171.1 5.0 %collective-permute-done.13.refs_4_ = bf16[1024,256]{1,0:T(8,128)(2,1)S(1)} collective-permute-done((bf16[1024,256]{1,0:T(8,128)(2,1)S(1)}, bf16[1024,256]{1,0:T(8,128)(2,1)S(1)}, u32[]{:S(2)}, u32[]{:S(2)}) %collective-permute-start.13) | collective-permute-done | bytes 524320 | tf_op jit(solution)/shard_map/ppermute | solution.py:48
  176.2 2.1 %collective-permute-done.12.refs_3_ = bf16[1024,256]{1,0:T(8,128)(2,1)S(1)} collective-permute-done((bf16[1024,256]{1,0:T(8,128)(2,1)S(1)}, bf16[1024,256]{1,0:T(8,128)(2,1)S(1)}, u32[]{:S(2)}, u32[]{:S(2)}) %collective-permute-start.12) | collective-permute-done | bytes 524320 | tf_op jit(solution)/shard_map/ppermute | solution.py:48
  178.3 0.0 copy-done.1
  178.3 2.2 %panel_products.3 = bf16[8,160,256]{2,1,0:T(8,128)(2,1)S(1)} custom-call(s32[8,16]{1,0:T(8,128)S(1)} %fusion.20.place_ref, bf16[16,8,128,128]{3,2,1,0:T(8,128)(2,1)S(1)} %bitcast.43, bf16[2112,256]{1,0:T(8,128)(2,1)S(1)} %get-tuple-element.26.refs_0_, bf16[2112,256]{1,0:T(8,128)(2,1)S(1)} %collective-permute-done.10.refs_1_, ...), custom_call_target="tpu_custom_call" | custom-call | flops 1073741824 | bytes 9437184 | tf_op jit(solution)/shard_map/panel_products/pallas_call | solution.py:160
  180.5 13.2 %all_to_all.16.received_ref = bf16[8,160,256]{2,1,0:T(8,128)(2,1)S(1)} all-to-all(bf16[8,160,256]{2,1,0:T(8,128)(2,1)S(1)} %broadcast_dynamic-update-slice_fusion), channel_id=1, replica_groups=mesh['X'=4,'ZH'=4,'ZL'=4,'Y'=4,'C'=2] {'Y','C'}, dimensions={0} | all-to-all | bytes 1310720 | tf_op jit(solution)/shard_map/all_to_all | solution.py:242
  193.8 0.8 tail.1
  (29 shorter events, 0.5 us)
Async XLA Ops:
  0.6 95.3 %copy-start = (bf16[256,256]{1,0:T(8,128)(2,1)S(1)}, bf16[256,256]{1,0:T(8,128)(2,1)}, u32[]{:S(2)}) copy-start(bf16[256,256]{1,0:T(8,128)(2,1)} %param.10) | copy-start | bytes 393220
  26.2 12.9 %collective-permute-start = (bf16[512,256]{1,0:T(8,128)(2,1)S(1)}, bf16[512,256]{1,0:T(8,128)(2,1)S(1)}, u32[]{:S(2)}, u32[]{:S(2)}) collective-permute-start(bf16[512,256]{1,0:T(8,128)(2,1)S(1)} %all-gather), channel_id=1, source_target_pairs={{264,0},{145,1},{272,8},{153,9},{280,16},{161,17},{288,24},{169,25... | collective-permute-start | bytes 786440 | tf_op jit(solution)/shard_map/ppermute | solution.py:48
  31.2 13.3 %collective-permute-start.1 = (bf16[512,256]{1,0:T(8,128)(2,1)S(1)}, bf16[512,256]{1,0:T(8,128)(2,1)S(1)}, u32[]{:S(2)}, u32[]{:S(2)}) collective-permute-start(bf16[512,256]{1,0:T(8,128)(2,1)S(1)} %all-gather), channel_id=1, source_target_pairs={{16,0},{257,1},{120,8},{265,9},{32,16},{273,17},{8,24},{281,25},{4... | collective-permute-start | bytes 786440 | tf_op jit(solution)/shard_map/ppermute | solution.py:48
  33.6 16.7 %collective-permute-start.2 = (bf16[512,256]{1,0:T(8,128)(2,1)S(1)}, bf16[512,256]{1,0:T(8,128)(2,1)S(1)}, u32[]{:S(2)}, u32[]{:S(2)}) collective-permute-start(bf16[512,256]{1,0:T(8,128)(2,1)S(1)} %all-gather), channel_id=1, source_target_pairs={{376,0},{497,1},{256,8},{505,9},{264,16},{385,17},{272,24},{393,25... | collective-permute-start | bytes 786440 | tf_op jit(solution)/shard_map/ppermute | solution.py:48
  50.3 26.5 %collective-permute-start.4 = (bf16[2048,256]{1,0:T(8,128)(2,1)S(1)}, bf16[2048,256]{1,0:T(8,128)(2,1)S(1)}, u32[]{:S(2)}, u32[]{:S(2)}) collective-permute-start(bf16[2048,256]{1,0:T(8,128)(2,1)S(1)} %constant_dynamic-update-slice_fusion.refs_0_), channel_id=1, source_target_pairs={{384,0},{121,1},{392,8},{1,9},{400,16},{9,17},{408,24},{17,25},{41... | collective-permute-start | bytes 3145736 | tf_op jit(solution)/shard_map/ppermute | solution.py:48
  54.5 22.3 %collective-permute-start.3 = (bf16[2048,256]{1,0:T(8,128)(2,1)S(1)}, bf16[2048,256]{1,0:T(8,128)(2,1)S(1)}, u32[]{:S(2)}, u32[]{:S(2)}) collective-permute-start(bf16[2048,256]{1,0:T(8,128)(2,1)S(1)} %constant_dynamic-update-slice_fusion.refs_0_), channel_id=1, source_target_pairs={{128,0},{9,1},{136,8},{17,9},{144,16},{25,17},{152,24},{33,25},{16... | collective-permute-start | bytes 3145736 | tf_op jit(solution)/shard_map/ppermute | solution.py:48
  58.3 17.2 %collective-permute-start.6 = (bf16[1024,256]{1,0:T(8,128)(2,1)}, bf16[1024,256]{1,0:T(8,128)(2,1)}, u32[]{:S(2)}, u32[]{:S(2)}) collective-permute-start(bf16[1024,256]{1,0:T(8,128)(2,1)} %constant_dynamic-update-slice_fusion.4), channel_id=1, source_target_pairs={{120,0},{385,1},{0,8},{393,9},{8,16},{401,17},{16,24},{409,25},{24... | collective-permute-start | bytes 1572872 | tf_op jit(solution)/shard_map/ppermute | solution.py:48
  60.2 16.6 %collective-permute-start.5 = (bf16[1024,256]{1,0:T(8,128)(2,1)}, bf16[1024,256]{1,0:T(8,128)(2,1)}, u32[]{:S(2)}, u32[]{:S(2)}) collective-permute-start(bf16[1024,256]{1,0:T(8,128)(2,1)} %constant_dynamic-update-slice_fusion.4), channel_id=1, source_target_pairs={{8,0},{129,1},{16,8},{137,9},{24,16},{145,17},{32,24},{153,25},{40... | collective-permute-start | bytes 1572872 | tf_op jit(solution)/shard_map/ppermute | solution.py:48
  64.8 2.2 %copy-start.2 = (s32[1,16,8]{1,2,0:T(8,128)S(1)}, s32[1,16,8]{1,2,0:T(8,128)}, u32[]{:S(2)}) copy-start(s32[1,16,8]{1,2,0:T(8,128)} %param.9) | copy-start | bytes 1540
  80.2 15.8 %copy-start.3 = (bf16[128,256]{1,0:T(8,128)(2,1)S(1)}, bf16[128,256]{1,0:T(8,128)(2,1)}, u32[]{:S(2)}) copy-start(bf16[128,256]{1,0:T(8,128)(2,1)} %param.11) | copy-start | bytes 196612
  97.1 9.6 %all-to-all-start.1 = ((bf16[8,32,256]{2,1,0:T(8,128)(2,1)}), bf16[8,32,256]{2,1,0:T(8,128)(2,1)S(1)}, u32[]{:S(2)}, u32[]{:S(2)}) async-start(bf16[8,32,256]{2,1,0:T(8,128)(2,1)} %bitcast.4), calls=%async_computation.1 | async-start | bytes 262144 | tf_op jit(solution)/shard_map/all_to_all | solution.py:236
  126.7 17.3 %collective-permute-start.9 = (bf16[576,256]{1,0:T(8,128)(2,1)S(1)}, bf16[576,256]{1,0:T(8,128)(2,1)S(1)}, u32[]{:S(2)}, u32[]{:S(2)}) collective-permute-start(bf16[576,256]{1,0:T(8,128)(2,1)S(1)} %pad_maximum_fusion), channel_id=1, source_target_pairs={{376,0},{497,1},{256,8},{505,9},{264,16},{385,17},{272,24},{393,25... | collective-permute-start | bytes 884744 | tf_op jit(solution)/shard_map/ppermute | solution.py:48
  128.6 15.6 %collective-permute-start.8 = (bf16[576,256]{1,0:T(8,128)(2,1)S(1)}, bf16[576,256]{1,0:T(8,128)(2,1)S(1)}, u32[]{:S(2)}, u32[]{:S(2)}) collective-permute-start(bf16[576,256]{1,0:T(8,128)(2,1)S(1)} %pad_maximum_fusion), channel_id=1, source_target_pairs={{16,0},{257,1},{120,8},{265,9},{32,16},{273,17},{8,24},{281,25},{4... | collective-permute-start | bytes 884744 | tf_op jit(solution)/shard_map/ppermute | solution.py:48
  133.0 15.4 %collective-permute-start.7 = (bf16[576,256]{1,0:T(8,128)(2,1)S(1)}, bf16[576,256]{1,0:T(8,128)(2,1)S(1)}, u32[]{:S(2)}, u32[]{:S(2)}) collective-permute-start(bf16[576,256]{1,0:T(8,128)(2,1)S(1)} %pad_maximum_fusion), channel_id=1, source_target_pairs={{264,0},{145,1},{272,8},{153,9},{280,16},{161,17},{288,24},{169,25... | collective-permute-start | bytes 884744 | tf_op jit(solution)/shard_map/ppermute | solution.py:48
  144.2 34.1 %copy-start.1 = (bf16[1,16,8,128,128]{4,3,2,1,0:T(8,128)(2,1)S(1)}, bf16[1,16,8,128,128]{4,3,2,1,0:T(8,128)(2,1)}, u32[]{:S(2)}) copy-start(bf16[1,16,8,128,128]{4,3,2,1,0:T(8,128)(2,1)} %param.8) | copy-start | bytes 12582916
  148.6 20.9 %collective-permute-start.11 = (bf16[2112,256]{1,0:T(8,128)(2,1)S(1)}, bf16[2112,256]{1,0:T(8,128)(2,1)S(1)}, u32[]{:S(2)}, u32[]{:S(2)}) collective-permute-start(bf16[2112,256]{1,0:T(8,128)(2,1)S(1)} %get-tuple-element.26.refs_0_), channel_id=1, source_target_pairs={{384,0},{121,1},{392,8},{1,9},{400,16},{9,17},{408,24},{17,25},{41... | collective-permute-start | bytes 3244040 | tf_op jit(solution)/shard_map/ppermute | solution.py:48
  152.5 18.6 %collective-permute-start.10 = (bf16[2112,256]{1,0:T(8,128)(2,1)S(1)}, bf16[2112,256]{1,0:T(8,128)(2,1)S(1)}, u32[]{:S(2)}, u32[]{:S(2)}) collective-permute-start(bf16[2112,256]{1,0:T(8,128)(2,1)S(1)} %get-tuple-element.26.refs_0_), channel_id=1, source_target_pairs={{128,0},{9,1},{136,8},{17,9},{144,16},{25,17},{152,24},{33,25},{16... | collective-permute-start | bytes 3244040 | tf_op jit(solution)/shard_map/ppermute | solution.py:48
  158.5 9.7 %collective-permute-start.14 = (bf16[64,256]{1,0:T(8,128)(2,1)S(1)}, bf16[64,256]{1,0:T(8,128)(2,1)S(1)}, u32[]{:S(2)}, u32[]{:S(2)}) collective-permute-start(bf16[64,256]{1,0:T(8,128)(2,1)S(1)} %get-tuple-element.34), channel_id=1, source_target_pairs={{8,0},{129,1},{16,8},{137,9},{24,16},{145,17},{32,24},{153,25},{40... | collective-permute-start | bytes 98312 | tf_op jit(solution)/shard_map/ppermute | solution.py:48
  161.7 14.5 %collective-permute-start.13 = (bf16[1024,256]{1,0:T(8,128)(2,1)S(1)}, bf16[1024,256]{1,0:T(8,128)(2,1)S(1)}, u32[]{:S(2)}, u32[]{:S(2)}) collective-permute-start(bf16[1024,256]{1,0:T(8,128)(2,1)S(1)} %constant_dynamic-update-slice_fusion.10), channel_id=1, source_target_pairs={{120,0},{385,1},{0,8},{393,9},{8,16},{401,17},{16,24},{409,25},{24... | collective-permute-start | bytes 1572872 | tf_op jit(solution)/shard_map/ppermute | solution.py:48
  163.8 14.5 %collective-permute-start.12 = (bf16[1024,256]{1,0:T(8,128)(2,1)S(1)}, bf16[1024,256]{1,0:T(8,128)(2,1)S(1)}, u32[]{:S(2)}, u32[]{:S(2)}) collective-permute-start(bf16[1024,256]{1,0:T(8,128)(2,1)S(1)} %constant_dynamic-update-slice_fusion.10), channel_id=1, source_target_pairs={{8,0},{129,1},{16,8},{137,9},{24,16},{145,17},{32,24},{153,25},{40... | collective-permute-start | bytes 1572872 | tf_op jit(solution)/shard_map/ppermute | solution.py:48

commit v3 on v2

--- a/solution.py
+++ b/solution.py
@@ -17,14 +17,14 @@
 
 SECOND = (((2, 1), (0, 2), (2, -1)), ((1, 2), (2, 0), (-1, -2)))
 THIRD = (((1, 0), (-1, 0), (0, 1), (0, -1)), ((0, 1), (0, -1), (1, 0), (-1, 0)))
-PIECES = (16, 16, 16, 8, 8)
+PIECES, EACH = 8, 8
 BLK = 128
 
 
 def place_table(core):
     held = ((0, 0),) + SECOND[core]
     table = {k: 4 * i for i, k in enumerate(held)}
-    at = PIECES[0]
+    at = 4 * len(held)
     for i, (dx, dz) in enumerate(THIRD[core]):
         sent = held if i < 2 else held[:2]
         for hx, hz in sent:
@@ -79,18 +79,20 @@
         for m in more:
             terms.append(whole(m[size:]))
         pair = halves((terms[0] + terms[2]) + (terms[1] + terms[3]))
-    held = stacked([own] + [m[:size] for m in more], pair)
-    half = jnp.concatenate(lax.optimization_barrier([own, more[0][:size]]), axis=0)
-    near = []
-    for i, steps in enumerate(zip(*THIRD)):
-        near.append(shift(held if i < 2 else half, *steps))
+    early = jnp.concatenate(lax.optimization_barrier([own, more[0][:size]]), axis=0)
+    late = stacked([m[:size] for m in more[1:]], pair)
+    near, rest = [], []
+    for steps in zip(*THIRD):
+        near.append(shift(early, *steps))
+    for steps in list(zip(*THIRD))[:2]:
+        rest.append(shift(late, *steps))
     total = None
     if riding is not None:
         side = whole(shift(pair, *list(zip(*THIRD))[2]))
         n = pair.shape[0]
-        plus, minus = (whole(v[-n:]) for v in near[:2])
+        plus, minus = (whole(v[-n:]) for v in rest)
         total = (whole(pair) + side) + (plus + minus)
-    return (held, *near), total
+    return (early, late, near[0], rest[0], near[1], rest[1], *near[2:]), total
 
 
 def places(columns):
@@ -124,17 +126,15 @@
 
 
 def product_kernel(place_ref, values_ref, *refs):
-    pieces, (out_ref, panels, piece_sem) = refs[:5], refs[5:]
+    pieces, (out_ref, panels, piece_sem) = refs[:PIECES], refs[PIECES:]
     rounds, rows, blk, _ = values_ref.shape
-    moves, at = [], 0
+    moves, n = [], EACH * blk
     for i, piece in enumerate(pieces):
-        n = PIECES[i] * blk
         moves.append(
             pltpu.make_async_copy(
-                piece.at[pl.ds(0, n)], panels.at[pl.ds(at, n)], piece_sem.at[i]
+                piece.at[pl.ds(0, n)], panels.at[pl.ds(i * n, n)], piece_sem.at[i]
             )
         )
-        at += n
     for move in moves:
         move.start()
     for move in moves:
@@ -164,11 +164,11 @@
             pl.BlockSpec(memory_space=pltpu.SMEM),
             pl.BlockSpec(memory_space=pltpu.VMEM),
         ]
-        + [any_space] * 5,
+        + [any_space] * PIECES,
         out_specs=pl.BlockSpec(memory_space=pltpu.VMEM),
         scratch_shapes=[
-            pltpu.VMEM((sum(PIECES) * blk, width), jnp.bfloat16),
-            pltpu.SemaphoreType.DMA((5,)),
+            pltpu.VMEM((PIECES * EACH * blk, width), jnp.bfloat16),
+            pltpu.SemaphoreType.DMA((PIECES,)),
         ],
         compiler_params=pltpu.CompilerParams(vmem_limit_bytes=20 * 2**20),
         cost_estimate=pl.CostEstimate(

time: 196 us -> 210 us (1.071)
  starting transfers between devices: 61.2 us -> 77.8 us
  waiting for transfers between devices: 46 us -> 39.7 us
  blocking collectives: 74.5 us -> 80.2 us
    ppermute x15 -> x19, starting transfers between devices: 56.9 us -> 73.4 us  [shift(): return lax.ppermute(value, DOM + ('C',), pairs)]
    ppermute x15 -> x19, waiting for transfers between devices: 40.9 us -> 34.6 us  [shift(): return lax.ppermute(value, DOM + ('C',), pairs)]
    all_to_all x1, blocking collectives: 15.7 us -> 22 us  [summed_over_rep(): received = lax.all_to_all(partial, REP, 0, 0, tiled=True)]
    all_gather x2, blocking collectives: 45.5 us -> 41.2 us  [gather_panels(): got = lax.all_gather(stacked([value], riding), 'ZH', axis=0, tiled=False)]
    all_to_all x1, blocking collectives: 13.2 us -> 16.9 us  [shards(): received = lax.all_to_all(back, REP, 0, 0, tiled=True)]
  transfers between devices with their start and end apart: 16 -> 20, of which waited for: 13 -> 10; matrix products, arithmetic and copies ran while one was open for 1% -> 0% of each run, Pallas kernels for 1% -> 1%
where the time goes in v3:
time: 210 us; the launch traced here: 209 us
  blocking collectives  80.2 us (38%)
  starting transfers between devices  77.8 us (37%)
  waiting for transfers between devices  39.7 us (19%)
  Pallas kernels  8.56 us (4%)
    ppermute x19, starting transfers between devices, shift(): return lax.ppermute(value, DOM + ('C',), pairs)  73.4 us
    all_gather x2, blocking collectives, gather_panels(): got = lax.all_gather(stacked([value], riding), 'ZH', axis=0, tiled=False)  41.2 us
    ppermute x19, waiting for transfers between devices, shift(): return lax.ppermute(value, DOM + ('C',), pairs)  34.6 us
    all_to_all x1, blocking collectives, summed_over_rep(): received = lax.all_to_all(partial, REP, 0, 0, tiled=True)  22 us
    all_to_all x1, blocking collectives, shards(): received = lax.all_to_all(back, REP, 0, 0, tiled=True)  16.9 us
    pallas_call x2, Pallas kernels, panel_products(): pl.pallas_call(product_kernel, out_shape=jax.ShapeDtypeStruct((rows, blk...  5.56 us
    all_to_all x1, waiting for transfers between devices, shards(): slices = lax.all_to_all(weight_part, REP, 0, 0, tiled=True)  5.07 us
    all_to_all x1, starting transfers between devices, shards(): slices = lax.all_to_all(weight_part, REP, 0, 0, tiled=True)  4.32 us
  transfers between devices with their start and end apart: 20, of which 10 were waited for; matrix products, arithmetic and copies ran while one was open for 0% of the time, Pallas kernels for 1%

profile of v3, /device:TPU:1, one launch (start us, length us, event | category | flops | bytes accessed | tf_op | source)
XLA Modules:
  0.0 209.1 jit_solution(7604004948718811549)
XLA Ops:
  0.6 0.0 copy-start
  0.6 25.6 %all-gather = bf16[512,256]{1,0:T(8,128)(2,1)S(1)} all-gather(bf16[128,256]{1,0:T(8,128)(2,1)} %param.7), channel_id=2, replica_groups=mesh['X'=4,'ZH'=4,'ZL'=4,'Y'=4,'C'=2] {'ZH'}, dimensions={0}, use_global_device_ids=true | all-gather | bytes 327680 | tf_op jit(solution)/shard_map/all_gather | solution.py:68
  26.2 4.9 %collective-permute-start = (bf16[512,256]{1,0:T(8,128)(2,1)S(1)}, bf16[512,256]{1,0:T(8,128)(2,1)S(1)}, u32[]{:S(2)}, u32[]{:S(2)}) collective-permute-start(bf16[512,256]{1,0:T(8,128)(2,1)S(1)} %all-gather), channel_id=1, source_target_pairs={{264,0},{145,1},{272,8},{153,9},{280,16},{161,17},{288,24},{169,25... | collective-permute-start | bytes 786440 | tf_op jit(solution)/shard_map/ppermute | solution.py:48
  31.2 7.9 %collective-permute-done = bf16[512,256]{1,0:T(8,128)(2,1)S(1)} collective-permute-done((bf16[512,256]{1,0:T(8,128)(2,1)S(1)}, bf16[512,256]{1,0:T(8,128)(2,1)S(1)}, u32[]{:S(2)}, u32[]{:S(2)}) %collective-permute-start) | collective-permute-done | bytes 262176 | tf_op jit(solution)/shard_map/ppermute | solution.py:48
  39.1 3.8 %collective-permute-start.8 = (bf16[1024,256]{1,0:T(8,128)(2,1)S(1)}, bf16[1024,256]{1,0:T(8,128)(2,1)S(1)}, u32[]{:S(2)}, u32[]{:S(2)}) collective-permute-start(bf16[1024,256]{1,0:T(8,128)(2,1)S(1)} %constant_dynamic-update-slice_fusion.refs_0_), channel_id=1, source_target_pairs={{120,0},{385,1},{0,8},{393,9},{8,16},{401,17},{16,24},{409,25},{24... | collective-permute-start | bytes 1572872 | tf_op jit(solution)/shard_map/ppermute | solution.py:48
  43.0 6.1 %collective-permute-start.1 = (bf16[512,256]{1,0:T(8,128)(2,1)S(1)}, bf16[512,256]{1,0:T(8,128)(2,1)S(1)}, u32[]{:S(2)}, u32[]{:S(2)}) collective-permute-start(bf16[512,256]{1,0:T(8,128)(2,1)S(1)} %all-gather), channel_id=1, source_target_pairs={{16,0},{257,1},{120,8},{265,9},{32,16},{273,17},{8,24},{281,25},{4... | collective-permute-start | bytes 786440 | tf_op jit(solution)/shard_map/ppermute | solution.py:48
  49.1 1.9 collective-permute-start.2
  51.0 4.5 %collective-permute-start.7 = (bf16[1024,256]{1,0:T(8,128)(2,1)S(1)}, bf16[1024,256]{1,0:T(8,128)(2,1)S(1)}, u32[]{:S(2)}, u32[]{:S(2)}) collective-permute-start(bf16[1024,256]{1,0:T(8,128)(2,1)S(1)} %constant_dynamic-update-slice_fusion.refs_0_), channel_id=1, source_target_pairs={{8,0},{129,1},{16,8},{137,9},{24,16},{145,17},{32,24},{153,25},{40... | collective-permute-start | bytes 1572872 | tf_op jit(solution)/shard_map/ppermute | solution.py:48
  55.5 4.5 %collective-permute-start.5 = (bf16[1024,256]{1,0:T(8,128)(2,1)S(1)}, bf16[1024,256]{1,0:T(8,128)(2,1)S(1)}, u32[]{:S(2)}, u32[]{:S(2)}) collective-permute-start(bf16[1024,256]{1,0:T(8,128)(2,1)S(1)} %constant_dynamic-update-slice_fusion.refs_0_), channel_id=1, source_target_pairs={{384,0},{121,1},{392,8},{1,9},{400,16},{9,17},{408,24},{17,25},{41... | collective-permute-start | bytes 1572872 | tf_op jit(solution)/shard_map/ppermute | solution.py:48
  60.0 0.0 collective-permute-done.1
  60.0 2.0 collective-permute-start.3
  62.1 5.7 %collective-permute-done.2 = bf16[512,256]{1,0:T(8,128)(2,1)S(1)} collective-permute-done((bf16[512,256]{1,0:T(8,128)(2,1)S(1)}, bf16[512,256]{1,0:T(8,128)(2,1)S(1)}, u32[]{:S(2)}, u32[]{:S(2)}) %collective-permute-start.2) | collective-permute-done | bytes 262176 | tf_op jit(solution)/shard_map/ppermute | solution.py:48
  67.8 1.9 collective-permute-start.6
  69.7 0.0 collective-permute-done.8.refs_7_
  69.7 4.6 %collective-permute-start.4 = (bf16[1024,256]{1,0:T(8,128)(2,1)S(1)}, bf16[1024,256]{1,0:T(8,128)(2,1)}, u32[]{:S(2)}, u32[]{:S(2)}) collective-permute-start(bf16[1024,256]{1,0:T(8,128)(2,1)S(1)} %constant_dynamic-update-slice_fusion.2.refs_1_), channel_id=1, source_target_pairs={{128,0},{9,1},{136,8},{17,9},{144,16},{25,17},{152,24},{33,25},{16... | collective-permute-start | bytes 1572872 | tf_op jit(solution)/shard_map/ppermute | solution.py:48
  74.4 0.0 copy-start.2
  74.4 2.2 %load_blocks.1.values_ref = bf16[16,8,128,128]{3,2,1,0:T(8,128)(2,1)S(1)} custom-call(bf16[16,8,128,128]{3,2,1,0:T(8,128)(2,1)} %bitcast.42), custom_call_target="tpu_custom_call" | custom-call | tf_op jit(solution)/shard_map/load_blocks/pallas_call | solution.py:117
  76.6 0.0 copy-done.2
  76.6 0.0 collective-permute-done.7.refs_6_
  76.6 0.0 collective-permute-done.5.refs_4_
  76.7 0.0 collective-permute-done.3.refs_2_
  76.7 2.4 %collective-permute-done.6.refs_5_ = bf16[1024,256]{1,0:T(8,128)(2,1)} collective-permute-done((bf16[1024,256]{1,0:T(8,128)(2,1)S(1)}, bf16[1024,256]{1,0:T(8,128)(2,1)}, u32[]{:S(2)}, u32[]{:S(2)}) %collective-permute-start.6) | collective-permute-done | bytes 524320 | tf_op jit(solution)/shard_map/ppermute | solution.py:48
  79.0 1.4 collective-permute-done.4.refs_3_
  80.4 3.3 %panel_products.2 = bf16[8,128,256]{2,1,0:T(8,128)(2,1)S(1)} custom-call(s32[8,16]{1,0:T(8,128)S(1)} %fusion.20.place_ref, bf16[16,8,128,128]{3,2,1,0:T(8,128)(2,1)S(1)} %load_blocks.1.values_ref, bf16[1024,256]{1,0:T(8,128)(2,1)S(1)} %constant_dynamic-update-slice_fusion.refs_0_, bf16[1024,256]{1,0:T(8,128)(2,1)S(1)} %constant_dynamic-update-slice_fusion.2.refs_1_, ...), custom_call_target="tpu_custom_call" | custom-call | flops 1073741824 | bytes 9437184 | tf_op jit(solution)/shard_map/panel_products/pallas_call | solution.py:160
  83.7 0.0 copy-start.3
  83.7 22.0 %all_to_all.15 = bf16[8,128,256]{2,1,0:T(8,128)(2,1)S(1)} all-to-all(bf16[8,128,256]{2,1,0:T(8,128)(2,1)S(1)} %panel_products.2), channel_id=1, replica_groups=mesh['X'=4,'ZH'=4,'ZL'=4,'Y'=4,'C'=2] {'Y','C'}, dimensions={0} | all-to-all | bytes 1048576 | tf_op jit(solution)/shard_map/all_to_all | solution.py:182
  105.8 0.1 reduce_sum.33
  105.8 0.0 copy-done
  105.9 0.0 copy-done.3
  105.9 0.2 multiply_convert_fusion
  106.1 0.9 convolution_convert_fusion
  106.9 4.3 %all-to-all-start.1 = ((bf16[8,32,256]{2,1,0:T(8,128)(2,1)}), bf16[8,32,256]{2,1,0:T(8,128)(2,1)S(1)}, u32[]{:S(2)}, u32[]{:S(2)}) async-start(bf16[8,32,256]{2,1,0:T(8,128)(2,1)} %bitcast.4), calls=%async_computation.1 | async-start | bytes 262144 | tf_op jit(solution)/shard_map/all_to_all | solution.py:236
  111.3 0.2 convolution_convert_fusion.1
  111.5 5.1 %all-to-all-done.1 = bf16[8,32,256]{2,1,0:T(8,128)(2,1)S(1)} async-done(((bf16[8,32,256]{2,1,0:T(8,128)(2,1)}), bf16[8,32,256]{2,1,0:T(8,128)(2,1)S(1)}, u32[]{:S(2)}, u32[]{:S(2)}) %all-to-all-start.1) | async-done | bytes 131104 | tf_op jit(solution)/shard_map/all_to_all | solution.py:236
  116.6 15.6 %all-gather.1 = bf16[640,256]{1,0:T(8,128)(2,1)S(1)} all-gather(bf16[160,256]{1,0:T(8,128)(2,1)S(1)} %pad_maximum_fusion.2), channel_id=3, replica_groups=mesh['X'=4,'ZH'=4,'ZL'=4,'Y'=4,'C'=2] {'ZH'}, dimensions={0}, use_global_device_ids=true | all-gather | bytes 409600 | tf_op jit(solution)/shard_map/all_gather | solution.py:68
  132.3 1.9 collective-permute-start.11
  134.2 5.6 %collective-permute-start.10 = (bf16[576,256]{1,0:T(8,128)(2,1)S(1)}, bf16[576,256]{1,0:T(8,128)(2,1)S(1)}, u32[]{:S(2)}, u32[]{:S(2)}) collective-permute-start(bf16[576,256]{1,0:T(8,128)(2,1)S(1)} %pad_maximum_fusion.1), channel_id=1, source_target_pairs={{16,0},{257,1},{120,8},{265,9},{32,16},{273,17},{8,24},{281,25},{4... | collective-permute-start | bytes 884744 | tf_op jit(solution)/shard_map/ppermute | solution.py:48
  139.8 7.0 %collective-permute-start.9 = (bf16[576,256]{1,0:T(8,128)(2,1)S(1)}, bf16[576,256]{1,0:T(8,128)(2,1)S(1)}, u32[]{:S(2)}, u32[]{:S(2)}) collective-permute-start(bf16[576,256]{1,0:T(8,128)(2,1)S(1)} %pad_maximum_fusion.1), channel_id=1, source_target_pairs={{264,0},{145,1},{272,8},{153,9},{280,16},{161,17},{288,24},{169,25... | collective-permute-start | bytes 884744 | tf_op jit(solution)/shard_map/ppermute | solution.py:48
  146.8 0.9 collective-permute-done.11
  147.7 3.9 %collective-permute-done.10 = bf16[576,256]{1,0:T(8,128)(2,1)S(1)} collective-permute-done((bf16[576,256]{1,0:T(8,128)(2,1)S(1)}, bf16[576,256]{1,0:T(8,128)(2,1)S(1)}, u32[]{:S(2)}, u32[]{:S(2)}) %collective-permute-start.10) | collective-permute-done | bytes 294944 | tf_op jit(solution)/shard_map/ppermute | solution.py:48
  151.6 4.2 %collective-permute-done.9 = bf16[576,256]{1,0:T(8,128)(2,1)S(1)} collective-permute-done((bf16[576,256]{1,0:T(8,128)(2,1)S(1)}, bf16[576,256]{1,0:T(8,128)(2,1)S(1)}, u32[]{:S(2)}, u32[]{:S(2)}) %collective-permute-start.9) | collective-permute-done | bytes 294944 | tf_op jit(solution)/shard_map/ppermute | solution.py:48
  155.8 0.0 copy-start.1
  155.9 2.7 %collective-permute-start.15 = (bf16[1088,256]{1,0:T(8,128)(2,1)S(1)}, bf16[1088,256]{1,0:T(8,128)(2,1)S(1)}, u32[]{:S(2)}, u32[]{:S(2)}) collective-permute-start(bf16[1088,256]{1,0:T(8,128)(2,1)S(1)} %pad_maximum_fusion.refs_1_), channel_id=1, source_target_pairs={{384,0},{121,1},{392,8},{1,9},{400,16},{9,17},{408,24},{17,25},{41... | collective-permute-start | bytes 1671176 | tf_op jit(solution)/shard_map/ppermute | solution.py:48
  158.6 4.3 %collective-permute-start.13 = (bf16[1088,256]{1,0:T(8,128)(2,1)S(1)}, bf16[1088,256]{1,0:T(8,128)(2,1)S(1)}, u32[]{:S(2)}, u32[]{:S(2)}) collective-permute-start(bf16[1088,256]{1,0:T(8,128)(2,1)S(1)} %pad_maximum_fusion.refs_1_), channel_id=1, source_target_pairs={{128,0},{9,1},{136,8},{17,9},{144,16},{25,17},{152,24},{33,25},{16... | collective-permute-start | bytes 1671176 | tf_op jit(solution)/shard_map/ppermute | solution.py:48
  162.9 4.8 %collective-permute-start.18 = (bf16[64,256]{1,0:T(8,128)(2,1)S(1)}, bf16[64,256]{1,0:T(8,128)(2,1)S(1)}, u32[]{:S(2)}, u32[]{:S(2)}) collective-permute-start(bf16[64,256]{1,0:T(8,128)(2,1)S(1)} %get-tuple-element.29), channel_id=1, source_target_pairs={{8,0},{129,1},{16,8},{137,9},{24,16},{145,17},{32,24},{153,25},{40... | collective-permute-start | bytes 98312 | tf_op jit(solution)/shard_map/ppermute | solution.py:48
  167.7 1.9 collective-permute-start.17
  169.7 4.6 %collective-permute-start.16 = (bf16[1024,256]{1,0:T(8,128)(2,1)S(1)}, bf16[1024,256]{1,0:T(8,128)(2,1)S(1)}, u32[]{:S(2)}, u32[]{:S(2)}) collective-permute-start(bf16[1024,256]{1,0:T(8,128)(2,1)S(1)} %constant_dynamic-update-slice_fusion.4.refs_0_), channel_id=1, source_target_pairs={{8,0},{129,1},{16,8},{137,9},{24,16},{145,17},{32,24},{153,25},{40... | collective-permute-start | bytes 1572872 | tf_op jit(solution)/shard_map/ppermute | solution.py:48
  174.2 0.0 collective-permute-done.18
  174.3 4.6 %collective-permute-start.14 = (bf16[1024,256]{1,0:T(8,128)(2,1)S(1)}, bf16[1024,256]{1,0:T(8,128)(2,1)S(1)}, u32[]{:S(2)}, u32[]{:S(2)}) collective-permute-start(bf16[1024,256]{1,0:T(8,128)(2,1)S(1)} %constant_dynamic-update-slice_fusion.4.refs_0_), channel_id=1, source_target_pairs={{384,0},{121,1},{392,8},{1,9},{400,16},{9,17},{408,24},{17,25},{41... | collective-permute-start | bytes 1572872 | tf_op jit(solution)/shard_map/ppermute | solution.py:48
  178.9 0.0 collective-permute-done.15.refs_5_
  178.9 1.9 collective-permute-start.12
  180.8 0.0 collective-permute-done.13.refs_3_
  180.9 0.0 collective-permute-done.17.refs_7_
  180.9 0.0 collective-permute-done.16.refs_6_
  180.9 6.8 %collective-permute-done.14.refs_4_ = bf16[1024,256]{1,0:T(8,128)(2,1)S(1)} collective-permute-done((bf16[1024,256]{1,0:T(8,128)(2,1)S(1)}, bf16[1024,256]{1,0:T(8,128)(2,1)S(1)}, u32[]{:S(2)}, u32[]{:S(2)}) %collective-permute-start.14) | collective-permute-done | bytes 524320 | tf_op jit(solution)/shard_map/ppermute | solution.py:48
  187.7 1.5 collective-permute-done.12.refs_2_
  189.1 0.0 copy-done.1
  189.1 2.3 %panel_products.3 = bf16[8,160,256]{2,1,0:T(8,128)(2,1)S(1)} custom-call(s32[8,16]{1,0:T(8,128)S(1)} %fusion.20.place_ref, bf16[16,8,128,128]{3,2,1,0:T(8,128)(2,1)S(1)} %bitcast.43, bf16[1024,256]{1,0:T(8,128)(2,1)S(1)} %constant_dynamic-update-slice_fusion.4.refs_0_, bf16[1088,256]{1,0:T(8,128)(2,1)S(1)} %pad_maximum_fusion.refs_1_, ...), custom_call_target="tpu_custom_call" | custom-call | flops 1073741824 | bytes 9437184 | tf_op jit(solution)/shard_map/panel_products/pallas_call | solution.py:160
  191.4 16.9 %all_to_all.16.received_ref = bf16[8,160,256]{2,1,0:T(8,128)(2,1)S(1)} all-to-all(bf16[8,160,256]{2,1,0:T(8,128)(2,1)S(1)} %broadcast_dynamic-update-slice_fusion), channel_id=1, replica_groups=mesh['X'=4,'ZH'=4,'ZL'=4,'Y'=4,'C'=2] {'Y','C'}, dimensions={0} | all-to-all | bytes 1310720 | tf_op jit(solution)/shard_map/all_to_all | solution.py:242
  208.3 0.8 tail.1
  (29 shorter events, 0.5 us)
Async XLA Ops:
  0.6 105.2 %copy-start = (bf16[256,256]{1,0:T(8,128)(2,1)S(1)}, bf16[256,256]{1,0:T(8,128)(2,1)}, u32[]{:S(2)}) copy-start(bf16[256,256]{1,0:T(8,128)(2,1)} %param.10) | copy-start | bytes 393220
  26.2 12.9 %collective-permute-start = (bf16[512,256]{1,0:T(8,128)(2,1)S(1)}, bf16[512,256]{1,0:T(8,128)(2,1)S(1)}, u32[]{:S(2)}, u32[]{:S(2)}) collective-permute-start(bf16[512,256]{1,0:T(8,128)(2,1)S(1)} %all-gather), channel_id=1, source_target_pairs={{264,0},{145,1},{272,8},{153,9},{280,16},{161,17},{288,24},{169,25... | collective-permute-start | bytes 786440 | tf_op jit(solution)/shard_map/ppermute | solution.py:48
  39.1 30.6 %collective-permute-start.8 = (bf16[1024,256]{1,0:T(8,128)(2,1)S(1)}, bf16[1024,256]{1,0:T(8,128)(2,1)S(1)}, u32[]{:S(2)}, u32[]{:S(2)}) collective-permute-start(bf16[1024,256]{1,0:T(8,128)(2,1)S(1)} %constant_dynamic-update-slice_fusion.refs_0_), channel_id=1, source_target_pairs={{120,0},{385,1},{0,8},{393,9},{8,16},{401,17},{16,24},{409,25},{24... | collective-permute-start | bytes 1572872 | tf_op jit(solution)/shard_map/ppermute | solution.py:48
  43.0 17.0 %collective-permute-start.1 = (bf16[512,256]{1,0:T(8,128)(2,1)S(1)}, bf16[512,256]{1,0:T(8,128)(2,1)S(1)}, u32[]{:S(2)}, u32[]{:S(2)}) collective-permute-start(bf16[512,256]{1,0:T(8,128)(2,1)S(1)} %all-gather), channel_id=1, source_target_pairs={{16,0},{257,1},{120,8},{265,9},{32,16},{273,17},{8,24},{281,25},{4... | collective-permute-start | bytes 786440 | tf_op jit(solution)/shard_map/ppermute | solution.py:48
  49.1 18.7 %collective-permute-start.2 = (bf16[512,256]{1,0:T(8,128)(2,1)S(1)}, bf16[512,256]{1,0:T(8,128)(2,1)S(1)}, u32[]{:S(2)}, u32[]{:S(2)}) collective-permute-start(bf16[512,256]{1,0:T(8,128)(2,1)S(1)} %all-gather), channel_id=1, source_target_pairs={{376,0},{497,1},{256,8},{505,9},{264,16},{385,17},{272,24},{393,25... | collective-permute-start | bytes 786440 | tf_op jit(solution)/shard_map/ppermute | solution.py:48
  51.0 25.6 %collective-permute-start.7 = (bf16[1024,256]{1,0:T(8,128)(2,1)S(1)}, bf16[1024,256]{1,0:T(8,128)(2,1)S(1)}, u32[]{:S(2)}, u32[]{:S(2)}) collective-permute-start(bf16[1024,256]{1,0:T(8,128)(2,1)S(1)} %constant_dynamic-update-slice_fusion.refs_0_), channel_id=1, source_target_pairs={{8,0},{129,1},{16,8},{137,9},{24,16},{145,17},{32,24},{153,25},{40... | collective-permute-start | bytes 1572872 | tf_op jit(solution)/shard_map/ppermute | solution.py:48
  55.5 21.1 %collective-permute-start.5 = (bf16[1024,256]{1,0:T(8,128)(2,1)S(1)}, bf16[1024,256]{1,0:T(8,128)(2,1)S(1)}, u32[]{:S(2)}, u32[]{:S(2)}) collective-permute-start(bf16[1024,256]{1,0:T(8,128)(2,1)S(1)} %constant_dynamic-update-slice_fusion.refs_0_), channel_id=1, source_target_pairs={{384,0},{121,1},{392,8},{1,9},{400,16},{9,17},{408,24},{17,25},{41... | collective-permute-start | bytes 1572872 | tf_op jit(solution)/shard_map/ppermute | solution.py:48
  60.0 16.6 %collective-permute-start.3 = (bf16[1024,256]{1,0:T(8,128)(2,1)S(1)}, bf16[1024,256]{1,0:T(8,128)(2,1)S(1)}, u32[]{:S(2)}, u32[]{:S(2)}) collective-permute-start(bf16[1024,256]{1,0:T(8,128)(2,1)S(1)} %constant_dynamic-update-slice_fusion.refs_0_), channel_id=1, source_target_pairs={{128,0},{9,1},{136,8},{17,9},{144,16},{25,17},{152,24},{33,25},{16... | collective-permute-start | bytes 1572872 | tf_op jit(solution)/shard_map/ppermute | solution.py:48
  67.8 11.2 %collective-permute-start.6 = (bf16[1024,256]{1,0:T(8,128)(2,1)S(1)}, bf16[1024,256]{1,0:T(8,128)(2,1)}, u32[]{:S(2)}, u32[]{:S(2)}) collective-permute-start(bf16[1024,256]{1,0:T(8,128)(2,1)S(1)} %constant_dynamic-update-slice_fusion.2.refs_1_), channel_id=1, source_target_pairs={{384,0},{121,1},{392,8},{1,9},{400,16},{9,17},{408,24},{17,25},{41... | collective-permute-start | bytes 1572872 | tf_op jit(solution)/shard_map/ppermute | solution.py:48
  69.7 10.7 %collective-permute-start.4 = (bf16[1024,256]{1,0:T(8,128)(2,1)S(1)}, bf16[1024,256]{1,0:T(8,128)(2,1)}, u32[]{:S(2)}, u32[]{:S(2)}) collective-permute-start(bf16[1024,256]{1,0:T(8,128)(2,1)S(1)} %constant_dynamic-update-slice_fusion.2.refs_1_), channel_id=1, source_target_pairs={{128,0},{9,1},{136,8},{17,9},{144,16},{25,17},{152,24},{33,25},{16... | collective-permute-start | bytes 1572872 | tf_op jit(solution)/shard_map/ppermute | solution.py:48
  74.4 2.2 %copy-start.2 = (s32[1,16,8]{1,2,0:T(8,128)S(1)}, s32[1,16,8]{1,2,0:T(8,128)}, u32[]{:S(2)}) copy-start(s32[1,16,8]{1,2,0:T(8,128)} %param.9) | copy-start | bytes 1540
  83.7 22.1 %copy-start.3 = (bf16[128,256]{1,0:T(8,128)(2,1)S(1)}, bf16[128,256]{1,0:T(8,128)(2,1)}, u32[]{:S(2)}) copy-start(bf16[128,256]{1,0:T(8,128)(2,1)} %param.11) | copy-start | bytes 196612
  106.9 9.6 %all-to-all-start.1 = ((bf16[8,32,256]{2,1,0:T(8,128)(2,1)}), bf16[8,32,256]{2,1,0:T(8,128)(2,1)S(1)}, u32[]{:S(2)}, u32[]{:S(2)}) async-start(bf16[8,32,256]{2,1,0:T(8,128)(2,1)} %bitcast.4), calls=%async_computation.1 | async-start | bytes 262144 | tf_op jit(solution)/shard_map/all_to_all | solution.py:236
  132.3 15.4 %collective-permute-start.11 = (bf16[576,256]{1,0:T(8,128)(2,1)S(1)}, bf16[576,256]{1,0:T(8,128)(2,1)S(1)}, u32[]{:S(2)}, u32[]{:S(2)}) collective-permute-start(bf16[576,256]{1,0:T(8,128)(2,1)S(1)} %pad_maximum_fusion.1), channel_id=1, source_target_pairs={{376,0},{497,1},{256,8},{505,9},{264,16},{385,17},{272,24},{393,25... | collective-permute-start | bytes 884744 | tf_op jit(solution)/shard_map/ppermute | solution.py:48
  134.2 17.4 %collective-permute-start.10 = (bf16[576,256]{1,0:T(8,128)(2,1)S(1)}, bf16[576,256]{1,0:T(8,128)(2,1)S(1)}, u32[]{:S(2)}, u32[]{:S(2)}) collective-permute-start(bf16[576,256]{1,0:T(8,128)(2,1)S(1)} %pad_maximum_fusion.1), channel_id=1, source_target_pairs={{16,0},{257,1},{120,8},{265,9},{32,16},{273,17},{8,24},{281,25},{4... | collective-permute-start | bytes 884744 | tf_op jit(solution)/shard_map/ppermute | solution.py:48
  139.8 16.0 %collective-permute-start.9 = (bf16[576,256]{1,0:T(8,128)(2,1)S(1)}, bf16[576,256]{1,0:T(8,128)(2,1)S(1)}, u32[]{:S(2)}, u32[]{:S(2)}) collective-permute-start(bf16[576,256]{1,0:T(8,128)(2,1)S(1)} %pad_maximum_fusion.1), channel_id=1, source_target_pairs={{264,0},{145,1},{272,8},{153,9},{280,16},{161,17},{288,24},{169,25... | collective-permute-start | bytes 884744 | tf_op jit(solution)/shard_map/ppermute | solution.py:48
  155.8 33.3 %copy-start.1 = (bf16[1,16,8,128,128]{4,3,2,1,0:T(8,128)(2,1)S(1)}, bf16[1,16,8,128,128]{4,3,2,1,0:T(8,128)(2,1)}, u32[]{:S(2)}) copy-start(bf16[1,16,8,128,128]{4,3,2,1,0:T(8,128)(2,1)} %param.8) | copy-start | bytes 12582916
  155.9 23.0 %collective-permute-start.15 = (bf16[1088,256]{1,0:T(8,128)(2,1)S(1)}, bf16[1088,256]{1,0:T(8,128)(2,1)S(1)}, u32[]{:S(2)}, u32[]{:S(2)}) collective-permute-start(bf16[1088,256]{1,0:T(8,128)(2,1)S(1)} %pad_maximum_fusion.refs_1_), channel_id=1, source_target_pairs={{384,0},{121,1},{392,8},{1,9},{400,16},{9,17},{408,24},{17,25},{41... | collective-permute-start | bytes 1671176 | tf_op jit(solution)/shard_map/ppermute | solution.py:48
  158.6 22.2 %collective-permute-start.13 = (bf16[1088,256]{1,0:T(8,128)(2,1)S(1)}, bf16[1088,256]{1,0:T(8,128)(2,1)S(1)}, u32[]{:S(2)}, u32[]{:S(2)}) collective-permute-start(bf16[1088,256]{1,0:T(8,128)(2,1)S(1)} %pad_maximum_fusion.refs_1_), channel_id=1, source_target_pairs={{128,0},{9,1},{136,8},{17,9},{144,16},{25,17},{152,24},{33,25},{16... | collective-permute-start | bytes 1671176 | tf_op jit(solution)/shard_map/ppermute | solution.py:48
  162.9 11.4 %collective-permute-start.18 = (bf16[64,256]{1,0:T(8,128)(2,1)S(1)}, bf16[64,256]{1,0:T(8,128)(2,1)S(1)}, u32[]{:S(2)}, u32[]{:S(2)}) collective-permute-start(bf16[64,256]{1,0:T(8,128)(2,1)S(1)} %get-tuple-element.29), channel_id=1, source_target_pairs={{8,0},{129,1},{16,8},{137,9},{24,16},{145,17},{32,24},{153,25},{40... | collective-permute-start | bytes 98312 | tf_op jit(solution)/shard_map/ppermute | solution.py:48
  167.7 13.1 %collective-permute-start.17 = (bf16[1024,256]{1,0:T(8,128)(2,1)S(1)}, bf16[1024,256]{1,0:T(8,128)(2,1)S(1)}, u32[]{:S(2)}, u32[]{:S(2)}) collective-permute-start(bf16[1024,256]{1,0:T(8,128)(2,1)S(1)} %constant_dynamic-update-slice_fusion.4.refs_0_), channel_id=1, source_target_pairs={{120,0},{385,1},{0,8},{393,9},{8,16},{401,17},{16,24},{409,25},{24... | collective-permute-start | bytes 1572872 | tf_op jit(solution)/shard_map/ppermute | solution.py:48
  169.7 11.2 %collective-permute-start.16 = (bf16[1024,256]{1,0:T(8,128)(2,1)S(1)}, bf16[1024,256]{1,0:T(8,128)(2,1)S(1)}, u32[]{:S(2)}, u32[]{:S(2)}) collective-permute-start(bf16[1024,256]{1,0:T(8,128)(2,1)S(1)} %constant_dynamic-update-slice_fusion.4.refs_0_), channel_id=1, source_target_pairs={{8,0},{129,1},{16,8},{137,9},{24,16},{145,17},{32,24},{153,25},{40... | collective-permute-start | bytes 1572872 | tf_op jit(solution)/shard_map/ppermute | solution.py:48
  174.3 13.4 %collective-permute-start.14 = (bf16[1024,256]{1,0:T(8,128)(2,1)S(1)}, bf16[1024,256]{1,0:T(8,128)(2,1)S(1)}, u32[]{:S(2)}, u32[]{:S(2)}) collective-permute-start(bf16[1024,256]{1,0:T(8,128)(2,1)S(1)} %constant_dynamic-update-slice_fusion.4.refs_0_), channel_id=1, source_target_pairs={{384,0},{121,1},{392,8},{1,9},{400,16},{9,17},{408,24},{17,25},{41... | collective-permute-start | bytes 1572872 | tf_op jit(solution)/shard_map/ppermute | solution.py:48
  178.9 10.3 %collective-permute-start.12 = (bf16[1024,256]{1,0:T(8,128)(2,1)S(1)}, bf16[1024,256]{1,0:T(8,128)(2,1)S(1)}, u32[]{:S(2)}, u32[]{:S(2)}) collective-permute-start(bf16[1024,256]{1,0:T(8,128)(2,1)S(1)} %constant_dynamic-update-slice_fusion.4.refs_0_), channel_id=1, source_target_pairs={{128,0},{9,1},{136,8},{17,9},{144,16},{25,17},{152,24},{33,25},{16... | collective-permute-start | bytes 1572872 | tf_op jit(solution)/shard_map/ppermute | solution.py:48

commit v4 on v2

--- a/solution.py
+++ b/solution.py
@@ -17,14 +17,14 @@
 
 SECOND = (((2, 1), (0, 2), (2, -1)), ((1, 2), (2, 0), (-1, -2)))
 THIRD = (((1, 0), (-1, 0), (0, 1), (0, -1)), ((0, 1), (0, -1), (1, 0), (-1, 0)))
-PIECES = (16, 16, 16, 8, 8)
+SPLIT, JOINED = (8,) * 8, (16, 16, 16, 8, 8)
 BLK = 128
 
 
 def place_table(core):
     held = ((0, 0),) + SECOND[core]
     table = {k: 4 * i for i, k in enumerate(held)}
-    at = PIECES[0]
+    at = 4 * len(held)
     for i, (dx, dz) in enumerate(THIRD[core]):
         sent = held if i < 2 else held[:2]
         for hx, hz in sent:
@@ -79,18 +79,21 @@
         for m in more:
             terms.append(whole(m[size:]))
         pair = halves((terms[0] + terms[2]) + (terms[1] + terms[3]))
-    held = stacked([own] + [m[:size] for m in more], pair)
-    half = jnp.concatenate(lax.optimization_barrier([own, more[0][:size]]), axis=0)
-    near = []
+    early = jnp.concatenate(lax.optimization_barrier([own, more[0][:size]]), axis=0)
+    parts = [m[:size] for m in more]
+    late = stacked(parts[1:] if riding is None else [own, *parts], pair)
+    large = early if riding is None else late
+    near, rest = [], []
     for i, steps in enumerate(zip(*THIRD)):
-        near.append(shift(held if i < 2 else half, *steps))
-    total = None
-    if riding is not None:
-        side = whole(shift(pair, *list(zip(*THIRD))[2]))
-        n = pair.shape[0]
-        plus, minus = (whole(v[-n:]) for v in near[:2])
-        total = (whole(pair) + side) + (plus + minus)
-    return (held, *near), total
+        near.append(shift(large if i < 2 else early, *steps))
+    if riding is None:
+        for steps in list(zip(*THIRD))[:2]:
+            rest.append(shift(late, *steps))
+        return (early, late, near[0], rest[0], near[1], rest[1], *near[2:]), None
+    side = whole(shift(pair, *list(zip(*THIRD))[2]))
+    n = pair.shape[0]
+    plus, minus = (whole(v[-n:]) for v in near[:2])
+    return (late, *near), (whole(pair) + side) + (plus + minus)
 
 
 def places(columns):
@@ -123,12 +126,12 @@
     )(pltpu.with_memory_space_constraint(values, pltpu.HBM))
 
 
-def product_kernel(place_ref, values_ref, *refs):
-    pieces, (out_ref, panels, piece_sem) = refs[:5], refs[5:]
+def product_kernel(sizes, place_ref, values_ref, *refs):
+    pieces, (out_ref, panels, piece_sem) = refs[: len(sizes)], refs[len(sizes) :]
     rounds, rows, blk, _ = values_ref.shape
     moves, at = [], 0
     for i, piece in enumerate(pieces):
-        n = PIECES[i] * blk
+        n = sizes[i] * blk
         moves.append(
             pltpu.make_async_copy(
                 piece.at[pl.ds(0, n)], panels.at[pl.ds(at, n)], piece_sem.at[i]
@@ -153,22 +156,22 @@
         out_ref[a, 0:blk] = total.astype(out_ref.dtype)
 
 
-def panel_products(values, place, pieces, spare=0):
+def panel_products(values, place, pieces, sizes, spare=0):
     rounds, rows, blk, _ = values.shape
     width = pieces[0].shape[-1]
     any_space = pl.BlockSpec(memory_space=pl.ANY)
     return pl.pallas_call(
-        product_kernel,
+        functools.partial(product_kernel, sizes),
         out_shape=jax.ShapeDtypeStruct((rows, blk + spare, width), jnp.bfloat16),
         in_specs=[
             pl.BlockSpec(memory_space=pltpu.SMEM),
             pl.BlockSpec(memory_space=pltpu.VMEM),
         ]
-        + [any_space] * 5,
+        + [any_space] * len(sizes),
         out_specs=pl.BlockSpec(memory_space=pltpu.VMEM),
         scratch_shapes=[
-            pltpu.VMEM((sum(PIECES) * blk, width), jnp.bfloat16),
-            pltpu.SemaphoreType.DMA((5,)),
+            pltpu.VMEM((sum(sizes) * blk, width), jnp.bfloat16),
+            pltpu.SemaphoreType.DMA((len(sizes),)),
         ],
         compiler_params=pltpu.CompilerParams(vmem_limit_bytes=20 * 2**20),
         cost_estimate=pl.CostEstimate(
@@ -228,7 +231,7 @@
     place = places(block_columns[0])
     panels, _ = gather_panels(features)
     blocks = loaded(values)
-    partial = panel_products(blocks, place, panels)
+    partial = panel_products(blocks, place, panels, SPLIT)
     hidden = summed_over_rep(partial).astype(jnp.bfloat16)
     hidden_grad, weight_part = dense_grads(hidden, weight, cotangent)
     n_rep = lax.axis_size(REP)
@@ -237,7 +240,7 @@
     weight_slice = jnp.sum(slices.astype(jnp.float32), axis=0).astype(jnp.bfloat16)
     panels, weight_slice = gather_panels(hidden_grad, weight_slice)
     extra = weight_slice.shape[0]
-    back = panel_products(values, place, panels, extra)
+    back = panel_products(values, place, panels, JOINED, extra)
     back = back.at[:, rows:].set(weight_slice.astype(jnp.bfloat16)[None])
     received = lax.all_to_all(back, REP, 0, 0, tiled=True)
     feature_grad, weight_grad = tail(received, rows, inv_scale)

time: 196 us -> 203 us (1.036)
  starting transfers between devices: 61.2 us -> 71 us
  waiting for transfers between devices: 46 us -> 41.9 us
  blocking collectives: 74.5 us -> 77.5 us
    ppermute x15 -> x17, starting transfers between devices: 56.9 us -> 66.7 us  [shift(): return lax.ppermute(value, DOM + ('C',), pairs)]
    all_to_all x1, blocking collectives: 15.7 us -> 22 us  [summed_over_rep(): received = lax.all_to_all(partial, REP, 0, 0, tiled=True)]
    all_gather x2, blocking collectives: 45.5 us -> 41.2 us  [gather_panels(): got = lax.all_gather(stacked([value], riding), 'ZH', axis=0, tiled=False)]
    ppermute x15 -> x17, waiting for transfers between devices: 40.9 us -> 36.8 us  [shift(): return lax.ppermute(value, DOM + ('C',), pairs)]
  transfers between devices with their start and end apart: 16 -> 18, of which waited for: 13 -> 11; matrix products, arithmetic and copies ran while one was open for 1% -> 0% of each run, Pallas kernels for 1% -> 1%
where the time goes in v4:
time: 203 us; the launch traced here: 202 us
  blocking collectives  77.5 us (38%)
  starting transfers between devices  71 us (35%)
  waiting for transfers between devices  41.9 us (21%)
  Pallas kernels  8.53 us (4%)
    ppermute x17, starting transfers between devices, shift(): return lax.ppermute(value, DOM + ('C',), pairs)  66.7 us
    all_gather x2, blocking collectives, gather_panels(): got = lax.all_gather(stacked([value], riding), 'ZH', axis=0, tiled=False)  41.2 us
    ppermute x17, waiting for transfers between devices, shift(): return lax.ppermute(value, DOM + ('C',), pairs)  36.8 us
    all_to_all x1, blocking collectives, summed_over_rep(): received = lax.all_to_all(partial, REP, 0, 0, tiled=True)  22 us
    all_to_all x1, blocking collectives, shards(): received = lax.all_to_all(back, REP, 0, 0, tiled=True)  14.3 us
    pallas_call x2, Pallas kernels, panel_products(): pl.pallas_call(functools.partial(product_kernel, sizes), out_shape=jax.Sh...  5.53 us
    all_to_all x1, waiting for transfers between devices, shards(): slices = lax.all_to_all(weight_part, REP, 0, 0, tiled=True)  5.07 us
    all_to_all x1, starting transfers between devices, shards(): slices = lax.all_to_all(weight_part, REP, 0, 0, tiled=True)  4.32 us
  transfers between devices with their start and end apart: 18, of which 11 were waited for; matrix products, arithmetic and copies ran while one was open for 0% of the time, Pallas kernels for 1%

profile of v4, /device:TPU:1, one launch (start us, length us, event | category | flops | bytes accessed | tf_op | source)
XLA Modules:
  0.0 201.9 jit_solution(1766355570868602282)
XLA Ops:
  0.6 0.0 copy-start
  0.6 25.6 %all-gather = bf16[512,256]{1,0:T(8,128)(2,1)S(1)} all-gather(bf16[128,256]{1,0:T(8,128)(2,1)} %param.7), channel_id=2, replica_groups=mesh['X'=4,'ZH'=4,'ZL'=4,'Y'=4,'C'=2] {'ZH'}, dimensions={0}, use_global_device_ids=true | all-gather | bytes 327680 | tf_op jit(solution)/shard_map/all_gather | solution.py:68
  26.2 4.9 %collective-permute-start = (bf16[512,256]{1,0:T(8,128)(2,1)S(1)}, bf16[512,256]{1,0:T(8,128)(2,1)S(1)}, u32[]{:S(2)}, u32[]{:S(2)}) collective-permute-start(bf16[512,256]{1,0:T(8,128)(2,1)S(1)} %all-gather), channel_id=1, source_target_pairs={{264,0},{145,1},{272,8},{153,9},{280,16},{161,17},{288,24},{169,25... | collective-permute-start | bytes 786440 | tf_op jit(solution)/shard_map/ppermute | solution.py:48
  31.2 7.9 %collective-permute-done = bf16[512,256]{1,0:T(8,128)(2,1)S(1)} collective-permute-done((bf16[512,256]{1,0:T(8,128)(2,1)S(1)}, bf16[512,256]{1,0:T(8,128)(2,1)S(1)}, u32[]{:S(2)}, u32[]{:S(2)}) %collective-permute-start) | collective-permute-done | bytes 262176 | tf_op jit(solution)/shard_map/ppermute | solution.py:48
  39.1 3.8 %collective-permute-start.8 = (bf16[1024,256]{1,0:T(8,128)(2,1)S(1)}, bf16[1024,256]{1,0:T(8,128)(2,1)S(1)}, u32[]{:S(2)}, u32[]{:S(2)}) collective-permute-start(bf16[1024,256]{1,0:T(8,128)(2,1)S(1)} %constant_dynamic-update-slice_fusion.refs_0_), channel_id=1, source_target_pairs={{120,0},{385,1},{0,8},{393,9},{8,16},{401,17},{16,24},{409,25},{24... | collective-permute-start | bytes 1572872 | tf_op jit(solution)/shard_map/ppermute | solution.py:48
  43.0 6.1 %collective-permute-start.1 = (bf16[512,256]{1,0:T(8,128)(2,1)S(1)}, bf16[512,256]{1,0:T(8,128)(2,1)S(1)}, u32[]{:S(2)}, u32[]{:S(2)}) collective-permute-start(bf16[512,256]{1,0:T(8,128)(2,1)S(1)} %all-gather), channel_id=1, source_target_pairs={{16,0},{257,1},{120,8},{265,9},{32,16},{273,17},{8,24},{281,25},{4... | collective-permute-start | bytes 786440 | tf_op jit(solution)/shard_map/ppermute | solution.py:48
  49.1 1.9 collective-permute-start.2
  51.0 4.5 %collective-permute-start.7 = (bf16[1024,256]{1,0:T(8,128)(2,1)S(1)}, bf16[1024,256]{1,0:T(8,128)(2,1)S(1)}, u32[]{:S(2)}, u32[]{:S(2)}) collective-permute-start(bf16[1024,256]{1,0:T(8,128)(2,1)S(1)} %constant_dynamic-update-slice_fusion.refs_0_), channel_id=1, source_target_pairs={{8,0},{129,1},{16,8},{137,9},{24,16},{145,17},{32,24},{153,25},{40... | collective-permute-start | bytes 1572872 | tf_op jit(solution)/shard_map/ppermute | solution.py:48
  55.5 4.5 %collective-permute-start.5 = (bf16[1024,256]{1,0:T(8,128)(2,1)S(1)}, bf16[1024,256]{1,0:T(8,128)(2,1)S(1)}, u32[]{:S(2)}, u32[]{:S(2)}) collective-permute-start(bf16[1024,256]{1,0:T(8,128)(2,1)S(1)} %constant_dynamic-update-slice_fusion.refs_0_), channel_id=1, source_target_pairs={{384,0},{121,1},{392,8},{1,9},{400,16},{9,17},{408,24},{17,25},{41... | collective-permute-start | bytes 1572872 | tf_op jit(solution)/shard_map/ppermute | solution.py:48
  60.0 0.0 collective-permute-done.1
  60.0 2.0 collective-permute-start.3
  62.1 5.7 %collective-permute-done.2 = bf16[512,256]{1,0:T(8,128)(2,1)S(1)} collective-permute-done((bf16[512,256]{1,0:T(8,128)(2,1)S(1)}, bf16[512,256]{1,0:T(8,128)(2,1)S(1)}, u32[]{:S(2)}, u32[]{:S(2)}) %collective-permute-start.2) | collective-permute-done | bytes 262176 | tf_op jit(solution)/shard_map/ppermute | solution.py:48
  67.8 1.9 collective-permute-start.6
  69.7 0.0 collective-permute-done.8.refs_7_
  69.7 4.6 %collective-permute-start.4 = (bf16[1024,256]{1,0:T(8,128)(2,1)S(1)}, bf16[1024,256]{1,0:T(8,128)(2,1)}, u32[]{:S(2)}, u32[]{:S(2)}) collective-permute-start(bf16[1024,256]{1,0:T(8,128)(2,1)S(1)} %constant_dynamic-update-slice_fusion.2.refs_1_), channel_id=1, source_target_pairs={{128,0},{9,1},{136,8},{17,9},{144,16},{25,17},{152,24},{33,25},{16... | collective-permute-start | bytes 1572872 | tf_op jit(solution)/shard_map/ppermute | solution.py:48
  74.4 0.0 copy-start.2
  74.4 2.2 %load_blocks.1.values_ref = bf16[16,8,128,128]{3,2,1,0:T(8,128)(2,1)S(1)} custom-call(bf16[16,8,128,128]{3,2,1,0:T(8,128)(2,1)} %bitcast.42), custom_call_target="tpu_custom_call" | custom-call | tf_op jit(solution)/shard_map/load_blocks/pallas_call | solution.py:118
  76.6 0.0 copy-done.2
  76.6 0.0 collective-permute-done.7.refs_6_
  76.6 0.0 collective-permute-done.5.refs_4_
  76.7 0.0 collective-permute-done.3.refs_2_
  76.7 2.4 %collective-permute-done.6.refs_5_ = bf16[1024,256]{1,0:T(8,128)(2,1)} collective-permute-done((bf16[1024,256]{1,0:T(8,128)(2,1)S(1)}, bf16[1024,256]{1,0:T(8,128)(2,1)}, u32[]{:S(2)}, u32[]{:S(2)}) %collective-permute-start.6) | collective-permute-done | bytes 524320 | tf_op jit(solution)/shard_map/ppermute | solution.py:48
  79.0 1.4 collective-permute-done.4.refs_3_
  80.4 3.3 %panel_products.2 = bf16[8,128,256]{2,1,0:T(8,128)(2,1)S(1)} custom-call(s32[8,16]{1,0:T(8,128)S(1)} %fusion.20.place_ref, bf16[16,8,128,128]{3,2,1,0:T(8,128)(2,1)S(1)} %load_blocks.1.values_ref, bf16[1024,256]{1,0:T(8,128)(2,1)S(1)} %constant_dynamic-update-slice_fusion.refs_0_, bf16[1024,256]{1,0:T(8,128)(2,1)S(1)} %constant_dynamic-update-slice_fusion.2.refs_1_, ...), custom_call_target="tpu_custom_call" | custom-call | flops 1073741824 | bytes 9437184 | tf_op jit(solution)/shard_map/panel_products/pallas_call | solution.py:163
  83.7 0.0 copy-start.3
  83.7 22.0 %all_to_all.15 = bf16[8,128,256]{2,1,0:T(8,128)(2,1)S(1)} all-to-all(bf16[8,128,256]{2,1,0:T(8,128)(2,1)S(1)} %panel_products.2), channel_id=1, replica_groups=mesh['X'=4,'ZH'=4,'ZL'=4,'Y'=4,'C'=2] {'Y','C'}, dimensions={0} | all-to-all | bytes 1048576 | tf_op jit(solution)/shard_map/all_to_all | solution.py:185
  105.8 0.1 reduce_sum.33
  105.8 0.0 copy-done
  105.9 0.0 copy-done.3
  105.9 0.2 multiply_convert_fusion
  106.1 0.9 convolution_convert_fusion
  106.9 4.3 %all-to-all-start.1 = ((bf16[8,32,256]{2,1,0:T(8,128)(2,1)}), bf16[8,32,256]{2,1,0:T(8,128)(2,1)S(1)}, u32[]{:S(2)}, u32[]{:S(2)}) async-start(bf16[8,32,256]{2,1,0:T(8,128)(2,1)} %bitcast.4), calls=%async_computation.1 | async-start | bytes 262144 | tf_op jit(solution)/shard_map/all_to_all | solution.py:239
  111.3 0.2 convolution_convert_fusion.1
  111.5 5.1 %all-to-all-done.1 = bf16[8,32,256]{2,1,0:T(8,128)(2,1)S(1)} async-done(((bf16[8,32,256]{2,1,0:T(8,128)(2,1)}), bf16[8,32,256]{2,1,0:T(8,128)(2,1)S(1)}, u32[]{:S(2)}, u32[]{:S(2)}) %all-to-all-start.1) | async-done | bytes 131104 | tf_op jit(solution)/shard_map/all_to_all | solution.py:239
  116.6 15.6 %all-gather.1 = bf16[640,256]{1,0:T(8,128)(2,1)S(1)} all-gather(bf16[160,256]{1,0:T(8,128)(2,1)S(1)} %pad_maximum_fusion.1), channel_id=3, replica_groups=mesh['X'=4,'ZH'=4,'ZL'=4,'Y'=4,'C'=2] {'ZH'}, dimensions={0}, use_global_device_ids=true | all-gather | bytes 409600 | tf_op jit(solution)/shard_map/all_gather | solution.py:68
  132.3 1.9 collective-permute-start.11
  134.2 5.6 %collective-permute-start.10 = (bf16[576,256]{1,0:T(8,128)(2,1)S(1)}, bf16[576,256]{1,0:T(8,128)(2,1)S(1)}, u32[]{:S(2)}, u32[]{:S(2)}) collective-permute-start(bf16[576,256]{1,0:T(8,128)(2,1)S(1)} %pad_maximum_fusion), channel_id=1, source_target_pairs={{16,0},{257,1},{120,8},{265,9},{32,16},{273,17},{8,24},{281,25},{4... | collective-permute-start | bytes 884744 | tf_op jit(solution)/shard_map/ppermute | solution.py:48
  139.8 7.0 %collective-permute-start.9 = (bf16[576,256]{1,0:T(8,128)(2,1)S(1)}, bf16[576,256]{1,0:T(8,128)(2,1)S(1)}, u32[]{:S(2)}, u32[]{:S(2)}) collective-permute-start(bf16[576,256]{1,0:T(8,128)(2,1)S(1)} %pad_maximum_fusion), channel_id=1, source_target_pairs={{264,0},{145,1},{272,8},{153,9},{280,16},{161,17},{288,24},{169,25... | collective-permute-start | bytes 884744 | tf_op jit(solution)/shard_map/ppermute | solution.py:48
  146.8 0.8 collective-permute-done.11
  147.7 3.9 %collective-permute-done.10 = bf16[576,256]{1,0:T(8,128)(2,1)S(1)} collective-permute-done((bf16[576,256]{1,0:T(8,128)(2,1)S(1)}, bf16[576,256]{1,0:T(8,128)(2,1)S(1)}, u32[]{:S(2)}, u32[]{:S(2)}) %collective-permute-start.10) | collective-permute-done | bytes 294944 | tf_op jit(solution)/shard_map/ppermute | solution.py:48
  151.6 0.0 copy-start.1
  151.6 4.2 %collective-permute-done.9 = bf16[576,256]{1,0:T(8,128)(2,1)S(1)} collective-permute-done((bf16[576,256]{1,0:T(8,128)(2,1)S(1)}, bf16[576,256]{1,0:T(8,128)(2,1)S(1)}, u32[]{:S(2)}, u32[]{:S(2)}) %collective-permute-start.9) | collective-permute-done | bytes 294944 | tf_op jit(solution)/shard_map/ppermute | solution.py:48
  155.9 2.4 %collective-permute-start.13 = (bf16[2112,256]{1,0:T(8,128)(2,1)S(1)}, bf16[2112,256]{1,0:T(8,128)(2,1)S(1)}, u32[]{:S(2)}, u32[]{:S(2)}) collective-permute-start(bf16[2112,256]{1,0:T(8,128)(2,1)S(1)} %get-tuple-element.26.refs_0_), channel_id=1, source_target_pairs={{384,0},{121,1},{392,8},{1,9},{400,16},{9,17},{408,24},{17,25},{41... | collective-permute-start | bytes 3244040 | tf_op jit(solution)/shard_map/ppermute | solution.py:48
  158.3 4.3 %collective-permute-start.12 = (bf16[2112,256]{1,0:T(8,128)(2,1)S(1)}, bf16[2112,256]{1,0:T(8,128)(2,1)S(1)}, u32[]{:S(2)}, u32[]{:S(2)}) collective-permute-start(bf16[2112,256]{1,0:T(8,128)(2,1)S(1)} %get-tuple-element.26.refs_0_), channel_id=1, source_target_pairs={{128,0},{9,1},{136,8},{17,9},{144,16},{25,17},{152,24},{33,25},{16... | collective-permute-start | bytes 3244040 | tf_op jit(solution)/shard_map/ppermute | solution.py:48
  162.6 4.8 %collective-permute-start.16 = (bf16[64,256]{1,0:T(8,128)(2,1)S(1)}, bf16[64,256]{1,0:T(8,128)(2,1)S(1)}, u32[]{:S(2)}, u32[]{:S(2)}) collective-permute-start(bf16[64,256]{1,0:T(8,128)(2,1)S(1)} %get-tuple-element.34), channel_id=1, source_target_pairs={{8,0},{129,1},{16,8},{137,9},{24,16},{145,17},{32,24},{153,25},{40... | collective-permute-start | bytes 98312 | tf_op jit(solution)/shard_map/ppermute | solution.py:48
  167.4 1.9 collective-permute-start.15
  169.4 4.6 %collective-permute-start.14 = (bf16[1024,256]{1,0:T(8,128)(2,1)S(1)}, bf16[1024,256]{1,0:T(8,128)(2,1)S(1)}, u32[]{:S(2)}, u32[]{:S(2)}) collective-permute-start(bf16[1024,256]{1,0:T(8,128)(2,1)S(1)} %constant_dynamic-update-slice_fusion.8), channel_id=1, source_target_pairs={{8,0},{129,1},{16,8},{137,9},{24,16},{145,17},{32,24},{153,25},{40... | collective-permute-start | bytes 1572872 | tf_op jit(solution)/shard_map/ppermute | solution.py:48
  173.9 0.0 collective-permute-done.16
  174.0 0.0 collective-permute-done.13.refs_2_
  174.0 2.7 %collective-permute-done.12.refs_1_ = bf16[2112,256]{1,0:T(8,128)(2,1)S(1)} collective-permute-done((bf16[2112,256]{1,0:T(8,128)(2,1)S(1)}, bf16[2112,256]{1,0:T(8,128)(2,1)S(1)}, u32[]{:S(2)}, u32[]{:S(2)}) %collective-permute-start.12) | collective-permute-done | bytes 1081376 | tf_op jit(solution)/shard_map/ppermute | solution.py:48
  176.7 5.7 %collective-permute-done.15.refs_4_ = bf16[1024,256]{1,0:T(8,128)(2,1)S(1)} collective-permute-done((bf16[1024,256]{1,0:T(8,128)(2,1)S(1)}, bf16[1024,256]{1,0:T(8,128)(2,1)S(1)}, u32[]{:S(2)}, u32[]{:S(2)}) %collective-permute-start.15) | collective-permute-done | bytes 524320 | tf_op jit(solution)/shard_map/ppermute | solution.py:48
  182.4 2.2 %collective-permute-done.14.refs_3_ = bf16[1024,256]{1,0:T(8,128)(2,1)S(1)} collective-permute-done((bf16[1024,256]{1,0:T(8,128)(2,1)S(1)}, bf16[1024,256]{1,0:T(8,128)(2,1)S(1)}, u32[]{:S(2)}, u32[]{:S(2)}) %collective-permute-start.14) | collective-permute-done | bytes 524320 | tf_op jit(solution)/shard_map/ppermute | solution.py:48
  184.6 0.0 copy-done.1
  184.6 2.2 %panel_products.3 = bf16[8,160,256]{2,1,0:T(8,128)(2,1)S(1)} custom-call(s32[8,16]{1,0:T(8,128)S(1)} %fusion.20.place_ref, bf16[16,8,128,128]{3,2,1,0:T(8,128)(2,1)S(1)} %bitcast.43, bf16[2112,256]{1,0:T(8,128)(2,1)S(1)} %get-tuple-element.26.refs_0_, bf16[2112,256]{1,0:T(8,128)(2,1)S(1)} %collective-permute-done.12.refs_1_, ...), custom_call_target="tpu_custom_call" | custom-call | flops 1073741824 | bytes 9437184 | tf_op jit(solution)/shard_map/panel_products/pallas_call | solution.py:163
  186.8 14.3 %all_to_all.16.received_ref = bf16[8,160,256]{2,1,0:T(8,128)(2,1)S(1)} all-to-all(bf16[8,160,256]{2,1,0:T(8,128)(2,1)S(1)} %broadcast_dynamic-update-slice_fusion), channel_id=1, replica_groups=mesh['X'=4,'ZH'=4,'ZL'=4,'Y'=4,'C'=2] {'Y','C'}, dimensions={0} | all-to-all | bytes 1310720 | tf_op jit(solution)/shard_map/all_to_all | solution.py:245
  201.1 0.8 tail.1
  (29 shorter events, 0.5 us)
Async XLA Ops:
  0.6 105.2 %copy-start = (bf16[256,256]{1,0:T(8,128)(2,1)S(1)}, bf16[256,256]{1,0:T(8,128)(2,1)}, u32[]{:S(2)}) copy-start(bf16[256,256]{1,0:T(8,128)(2,1)} %param.10) | copy-start | bytes 393220
  26.2 12.9 %collective-permute-start = (bf16[512,256]{1,0:T(8,128)(2,1)S(1)}, bf16[512,256]{1,0:T(8,128)(2,1)S(1)}, u32[]{:S(2)}, u32[]{:S(2)}) collective-permute-start(bf16[512,256]{1,0:T(8,128)(2,1)S(1)} %all-gather), channel_id=1, source_target_pairs={{264,0},{145,1},{272,8},{153,9},{280,16},{161,17},{288,24},{169,25... | collective-permute-start | bytes 786440 | tf_op jit(solution)/shard_map/ppermute | solution.py:48
  39.1 30.6 %collective-permute-start.8 = (bf16[1024,256]{1,0:T(8,128)(2,1)S(1)}, bf16[1024,256]{1,0:T(8,128)(2,1)S(1)}, u32[]{:S(2)}, u32[]{:S(2)}) collective-permute-start(bf16[1024,256]{1,0:T(8,128)(2,1)S(1)} %constant_dynamic-update-slice_fusion.refs_0_), channel_id=1, source_target_pairs={{120,0},{385,1},{0,8},{393,9},{8,16},{401,17},{16,24},{409,25},{24... | collective-permute-start | bytes 1572872 | tf_op jit(solution)/shard_map/ppermute | solution.py:48
  43.0 17.0 %collective-permute-start.1 = (bf16[512,256]{1,0:T(8,128)(2,1)S(1)}, bf16[512,256]{1,0:T(8,128)(2,1)S(1)}, u32[]{:S(2)}, u32[]{:S(2)}) collective-permute-start(bf16[512,256]{1,0:T(8,128)(2,1)S(1)} %all-gather), channel_id=1, source_target_pairs={{16,0},{257,1},{120,8},{265,9},{32,16},{273,17},{8,24},{281,25},{4... | collective-permute-start | bytes 786440 | tf_op jit(solution)/shard_map/ppermute | solution.py:48
  49.1 18.7 %collective-permute-start.2 = (bf16[512,256]{1,0:T(8,128)(2,1)S(1)}, bf16[512,256]{1,0:T(8,128)(2,1)S(1)}, u32[]{:S(2)}, u32[]{:S(2)}) collective-permute-start(bf16[512,256]{1,0:T(8,128)(2,1)S(1)} %all-gather), channel_id=1, source_target_pairs={{376,0},{497,1},{256,8},{505,9},{264,16},{385,17},{272,24},{393,25... | collective-permute-start | bytes 786440 | tf_op jit(solution)/shard_map/ppermute | solution.py:48
  51.0 25.6 %collective-permute-start.7 = (bf16[1024,256]{1,0:T(8,128)(2,1)S(1)}, bf16[1024,256]{1,0:T(8,128)(2,1)S(1)}, u32[]{:S(2)}, u32[]{:S(2)}) collective-permute-start(bf16[1024,256]{1,0:T(8,128)(2,1)S(1)} %constant_dynamic-update-slice_fusion.refs_0_), channel_id=1, source_target_pairs={{8,0},{129,1},{16,8},{137,9},{24,16},{145,17},{32,24},{153,25},{40... | collective-permute-start | bytes 1572872 | tf_op jit(solution)/shard_map/ppermute | solution.py:48
  55.5 21.1 %collective-permute-start.5 = (bf16[1024,256]{1,0:T(8,128)(2,1)S(1)}, bf16[1024,256]{1,0:T(8,128)(2,1)S(1)}, u32[]{:S(2)}, u32[]{:S(2)}) collective-permute-start(bf16[1024,256]{1,0:T(8,128)(2,1)S(1)} %constant_dynamic-update-slice_fusion.refs_0_), channel_id=1, source_target_pairs={{384,0},{121,1},{392,8},{1,9},{400,16},{9,17},{408,24},{17,25},{41... | collective-permute-start | bytes 1572872 | tf_op jit(solution)/shard_map/ppermute | solution.py:48
  60.0 16.6 %collective-permute-start.3 = (bf16[1024,256]{1,0:T(8,128)(2,1)S(1)}, bf16[1024,256]{1,0:T(8,128)(2,1)S(1)}, u32[]{:S(2)}, u32[]{:S(2)}) collective-permute-start(bf16[1024,256]{1,0:T(8,128)(2,1)S(1)} %constant_dynamic-update-slice_fusion.refs_0_), channel_id=1, source_target_pairs={{128,0},{9,1},{136,8},{17,9},{144,16},{25,17},{152,24},{33,25},{16... | collective-permute-start | bytes 1572872 | tf_op jit(solution)/shard_map/ppermute | solution.py:48
  67.8 11.2 %collective-permute-start.6 = (bf16[1024,256]{1,0:T(8,128)(2,1)S(1)}, bf16[1024,256]{1,0:T(8,128)(2,1)}, u32[]{:S(2)}, u32[]{:S(2)}) collective-permute-start(bf16[1024,256]{1,0:T(8,128)(2,1)S(1)} %constant_dynamic-update-slice_fusion.2.refs_1_), channel_id=1, source_target_pairs={{384,0},{121,1},{392,8},{1,9},{400,16},{9,17},{408,24},{17,25},{41... | collective-permute-start | bytes 1572872 | tf_op jit(solution)/shard_map/ppermute | solution.py:48
  69.7 10.7 %collective-permute-start.4 = (bf16[1024,256]{1,0:T(8,128)(2,1)S(1)}, bf16[1024,256]{1,0:T(8,128)(2,1)}, u32[]{:S(2)}, u32[]{:S(2)}) collective-permute-start(bf16[1024,256]{1,0:T(8,128)(2,1)S(1)} %constant_dynamic-update-slice_fusion.2.refs_1_), channel_id=1, source_target_pairs={{128,0},{9,1},{136,8},{17,9},{144,16},{25,17},{152,24},{33,25},{16... | collective-permute-start | bytes 1572872 | tf_op jit(solution)/shard_map/ppermute | solution.py:48
  74.4 2.2 %copy-start.2 = (s32[1,16,8]{1,2,0:T(8,128)S(1)}, s32[1,16,8]{1,2,0:T(8,128)}, u32[]{:S(2)}) copy-start(s32[1,16,8]{1,2,0:T(8,128)} %param.9) | copy-start | bytes 1540
  83.7 22.1 %copy-start.3 = (bf16[128,256]{1,0:T(8,128)(2,1)S(1)}, bf16[128,256]{1,0:T(8,128)(2,1)}, u32[]{:S(2)}) copy-start(bf16[128,256]{1,0:T(8,128)(2,1)} %param.11) | copy-start | bytes 196612
  106.9 9.6 %all-to-all-start.1 = ((bf16[8,32,256]{2,1,0:T(8,128)(2,1)}), bf16[8,32,256]{2,1,0:T(8,128)(2,1)S(1)}, u32[]{:S(2)}, u32[]{:S(2)}) async-start(bf16[8,32,256]{2,1,0:T(8,128)(2,1)} %bitcast.4), calls=%async_computation.1 | async-start | bytes 262144 | tf_op jit(solution)/shard_map/all_to_all | solution.py:239
  132.3 15.4 %collective-permute-start.11 = (bf16[576,256]{1,0:T(8,128)(2,1)S(1)}, bf16[576,256]{1,0:T(8,128)(2,1)S(1)}, u32[]{:S(2)}, u32[]{:S(2)}) collective-permute-start(bf16[576,256]{1,0:T(8,128)(2,1)S(1)} %pad_maximum_fusion), channel_id=1, source_target_pairs={{376,0},{497,1},{256,8},{505,9},{264,16},{385,17},{272,24},{393,25... | collective-permute-start | bytes 884744 | tf_op jit(solution)/shard_map/ppermute | solution.py:48
  134.2 17.4 %collective-permute-start.10 = (bf16[576,256]{1,0:T(8,128)(2,1)S(1)}, bf16[576,256]{1,0:T(8,128)(2,1)S(1)}, u32[]{:S(2)}, u32[]{:S(2)}) collective-permute-start(bf16[576,256]{1,0:T(8,128)(2,1)S(1)} %pad_maximum_fusion), channel_id=1, source_target_pairs={{16,0},{257,1},{120,8},{265,9},{32,16},{273,17},{8,24},{281,25},{4... | collective-permute-start | bytes 884744 | tf_op jit(solution)/shard_map/ppermute | solution.py:48
  139.8 16.0 %collective-permute-start.9 = (bf16[576,256]{1,0:T(8,128)(2,1)S(1)}, bf16[576,256]{1,0:T(8,128)(2,1)S(1)}, u32[]{:S(2)}, u32[]{:S(2)}) collective-permute-start(bf16[576,256]{1,0:T(8,128)(2,1)S(1)} %pad_maximum_fusion), channel_id=1, source_target_pairs={{264,0},{145,1},{272,8},{153,9},{280,16},{161,17},{288,24},{169,25... | collective-permute-start | bytes 884744 | tf_op jit(solution)/shard_map/ppermute | solution.py:48
  151.6 33.0 %copy-start.1 = (bf16[1,16,8,128,128]{4,3,2,1,0:T(8,128)(2,1)S(1)}, bf16[1,16,8,128,128]{4,3,2,1,0:T(8,128)(2,1)}, u32[]{:S(2)}) copy-start(bf16[1,16,8,128,128]{4,3,2,1,0:T(8,128)(2,1)} %param.8) | copy-start | bytes 12582916
  155.9 18.1 %collective-permute-start.13 = (bf16[2112,256]{1,0:T(8,128)(2,1)S(1)}, bf16[2112,256]{1,0:T(8,128)(2,1)S(1)}, u32[]{:S(2)}, u32[]{:S(2)}) collective-permute-start(bf16[2112,256]{1,0:T(8,128)(2,1)S(1)} %get-tuple-element.26.refs_0_), channel_id=1, source_target_pairs={{384,0},{121,1},{392,8},{1,9},{400,16},{9,17},{408,24},{17,25},{41... | collective-permute-start | bytes 3244040 | tf_op jit(solution)/shard_map/ppermute | solution.py:48
  158.3 18.4 %collective-permute-start.12 = (bf16[2112,256]{1,0:T(8,128)(2,1)S(1)}, bf16[2112,256]{1,0:T(8,128)(2,1)S(1)}, u32[]{:S(2)}, u32[]{:S(2)}) collective-permute-start(bf16[2112,256]{1,0:T(8,128)(2,1)S(1)} %get-tuple-element.26.refs_0_), channel_id=1, source_target_pairs={{128,0},{9,1},{136,8},{17,9},{144,16},{25,17},{152,24},{33,25},{16... | collective-permute-start | bytes 3244040 | tf_op jit(solution)/shard_map/ppermute | solution.py:48
  162.6 11.4 %collective-permute-start.16 = (bf16[64,256]{1,0:T(8,128)(2,1)S(1)}, bf16[64,256]{1,0:T(8,128)(2,1)S(1)}, u32[]{:S(2)}, u32[]{:S(2)}) collective-permute-start(bf16[64,256]{1,0:T(8,128)(2,1)S(1)} %get-tuple-element.34), channel_id=1, source_target_pairs={{8,0},{129,1},{16,8},{137,9},{24,16},{145,17},{32,24},{153,25},{40... | collective-permute-start | bytes 98312 | tf_op jit(solution)/shard_map/ppermute | solution.py:48
  167.4 15.0 %collective-permute-start.15 = (bf16[1024,256]{1,0:T(8,128)(2,1)S(1)}, bf16[1024,256]{1,0:T(8,128)(2,1)S(1)}, u32[]{:S(2)}, u32[]{:S(2)}) collective-permute-start(bf16[1024,256]{1,0:T(8,128)(2,1)S(1)} %constant_dynamic-update-slice_fusion.8), channel_id=1, source_target_pairs={{120,0},{385,1},{0,8},{393,9},{8,16},{401,17},{16,24},{409,25},{24... | collective-permute-start | bytes 1572872 | tf_op jit(solution)/shard_map/ppermute | solution.py:48
  169.4 15.2 %collective-permute-start.14 = (bf16[1024,256]{1,0:T(8,128)(2,1)S(1)}, bf16[1024,256]{1,0:T(8,128)(2,1)S(1)}, u32[]{:S(2)}, u32[]{:S(2)}) collective-permute-start(bf16[1024,256]{1,0:T(8,128)(2,1)S(1)} %constant_dynamic-update-slice_fusion.8), channel_id=1, source_target_pairs={{8,0},{129,1},{16,8},{137,9},{24,16},{145,17},{32,24},{153,25},{40... | collective-permute-start | bytes 1572872 | tf_op jit(solution)/shard_map/ppermute | solution.py:48
